TPU v7x, 256 devices: a whole 4x4x8 slice. The times are simulated.
256 devices in a mesh: seq: 64 (over z, y, core), tp: 4 (over x).
Axes of the slice: x: 4, y: 4, z: 8, core: 2. Of those that a mesh axis runs over, the one named last changes fastest.
Arguments:
- probe_vectors: bfloat16 [32768, 8192], P('seq', 'tp'), may hold values from -6 to 6
- lookup_vectors: bfloat16 [32768, 8192], P('seq', 'tp'), may hold values from -0.5 to 0.5
- payload_vectors: bfloat16 [32768, 8192], P('seq', 'tp'), may hold values from -400 to 400
- attender_fading_pace: float32 [64], P('tp'), may hold values from 0 to 0.034, as said below
- surplus_fading: float32 [32768, 64], P('seq', 'tp'), may hold values from -0.7 to 0, as said below
- normalizer_scaling: float32 [8192], P('tp'), may hold values from 0.25 to 1.75
Outputs:
- attended: bfloat16 [32768, 8192], P('seq', 'tp')
- final_state: float32 [64, 16384], P('tp', 'seq')
Inputs may be any that keep to these rules, and one draw needn't show every extreme that they name: `attender_fading_pace`: positive per-token decay rates; some heads forget within some tens of tokens. `surplus_fading`: zero at most tokens.
All inputs are finite; a program needn't handle non-finite values.
Results may differ from a plain program's by a relative error of at most 0.0031.
Values sent between devices are 32-bit elements; how exact they have to be, the bound alone decides.
No kernel may reach another device: no remote copies, remote signals or barrier semaphores. Data moves between devices by JAX's collectives and lax.ppermute only.
A program may use at most 192 MiB of HBM per device.

v0:
```python
import functools

import jax
import jax.numpy as jnp
from jax import lax
from jax.experimental import pallas as pl
from jax.experimental.pallas import tpu as pltpu
from jax.sharding import Mesh
from jax.sharding import PartitionSpec as P

HEAD_DIM = 128
BLOCK = 256
D = 8192
SEQ = ("seq_0", "seq_1", "seq_2")
CHIPS = ("seq_0", "seq_1")
CORE = "seq_2"
HEADS_HERE = 16
TOKENS_HERE = 512
GROUP = 4
GROUPS = HEADS_HERE // GROUP
CHIP_COUNT = 32
PIECE = 32
F32 = jnp.float32
BF16 = jnp.bfloat16


def dot(a, b, dims=((1,), (0,))):
    return lax.dot_general(a, b, (dims, ((), ())), preferred_element_type=F32)


def split(x):
    high = x.astype(BF16)
    return high, (x - high.astype(F32)).astype(BF16)


def log_decay(fading, pace):
    heads, tokens = fading.shape
    row = lax.broadcasted_iota(jnp.int32, (heads, heads), 0)
    col = lax.broadcasted_iota(jnp.int32, (heads, heads), 1)
    pace_column = jnp.sum(
        jnp.where(row == col, jnp.broadcast_to(pace, (heads, heads)), 0.0), axis=1, keepdims=True
    )
    c = fading - pace_column
    lane = lax.broadcasted_iota(jnp.int32, (heads, tokens), 1)
    shift = 1
    while shift < tokens:
        c = c + jnp.where(lane >= shift, pltpu.roll(c, shift, axis=1), 0.0)
        shift *= 2
    return c


def to_columns(rows):
    heads, tokens = rows.shape
    full = jnp.concatenate([rows, jnp.zeros((128 - heads, tokens), F32)], axis=0)
    return full.T


def total_row(c):
    heads = c.shape[0]
    last = jnp.broadcast_to(c[:, -1:], (heads, 128))
    row = lax.broadcasted_iota(jnp.int32, (heads, 128), 0)
    lane = lax.broadcasted_iota(jnp.int32, (heads, 128), 1)
    return jnp.sum(jnp.where(row == lane, last, 0.0), axis=0, keepdims=True)


def piece_column(row):
    r = lax.broadcasted_iota(jnp.int32, (PIECE, 128), 0)
    lane = lax.broadcasted_iota(jnp.int32, (PIECE, 128), 1)
    picked = jnp.where(lane == r // 2, jnp.broadcast_to(row, (PIECE, 128)), 0.0)
    return jnp.broadcast_to(jnp.sum(picked, axis=1, keepdims=True), (PIECE, 128))


def shuffle(x):
    sub = lax.broadcasted_iota(jnp.int32, x[0].shape, 1)
    for step in (1, 2):
        upper = ((sub // 2) & step) != 0
        y = list(x)
        for a in range(4):
            if a & step:
                continue
            b = a + step
            y[a] = jnp.where(upper, pltpu.roll(x[b], 2 * step, axis=1), x[a])
            y[b] = jnp.where(upper, x[b], pltpu.roll(x[a], 8 - 2 * step, axis=1))
        x = y
    return x


def state_kernel(k_ref, v_ref, fading_ref, pace_ref, keep_ref, send_ref, w_ref):
    g = pl.program_id(0)
    mine = lax.axis_index(CORE)

    @pl.when(g == 0)
    def _():
        c = log_decay(fading_ref[...], pace_ref[...])
        w_ref[...] = jnp.exp(c[:, -1:] - c)
        total = jnp.broadcast_to(total_row(c), (8, 128))
        keep_ref[pl.ds(CHIP_COUNT * PIECE, 8), :] = total
        send_ref[pl.ds(CHIP_COUNT * PIECE, 8), :] = total

    states = []
    for i in range(GROUP):
        lanes = slice(i * HEAD_DIM, (i + 1) * HEAD_DIM)
        turned = k_ref[:, lanes].T.astype(F32)
        decayed = turned * w_ref[pl.ds(g * GROUP + i, 1), :]
        high, low = split(decayed)
        both = dot(jnp.concatenate([high, low], axis=0), v_ref[:, lanes])
        state = both[:HEAD_DIM] + both[HEAD_DIM:]
        states.append(state.reshape(16, 8, 128))
    units = shuffle(states)
    for b in range(2):
        even, odd = units[2 * b], units[2 * b + 1]
        kept = jnp.where(mine == 0, even, odd)
        sent = jnp.where(mine == 0, odd, even)
        for j in range(16):
            at = pl.ds(pl.multiple_of((2 * j + b) * PIECE + g * 8, 8), 8)
            keep_ref[at, :] = kept[j]
            send_ref[at, :] = sent[j]


def local_states(k, v, fading, pace):
    rows = CHIP_COUNT * PIECE + 8
    return pl.pallas_call(
        state_kernel,
        grid=(GROUPS,),
        in_specs=[
            pl.BlockSpec((TOKENS_HERE, GROUP * HEAD_DIM), lambda g: (0, g)),
            pl.BlockSpec((TOKENS_HERE, GROUP * HEAD_DIM), lambda g: (0, g)),
            pl.BlockSpec((HEADS_HERE, TOKENS_HERE), lambda g: (0, 0)),
            pl.BlockSpec((1, HEADS_HERE), lambda g: (0, 0)),
        ],
        out_specs=[
            pl.BlockSpec((rows, 128), lambda g: (0, 0)),
            pl.BlockSpec((rows, 128), lambda g: (0, 0)),
        ],
        out_shape=[
            jax.ShapeDtypeStruct((rows, 128), F32),
            jax.ShapeDtypeStruct((rows, 128), F32),
        ],
        scratch_shapes=[pltpu.VMEM((HEADS_HERE, TOKENS_HERE), F32)],
        compiler_params=pltpu.CompilerParams(vmem_limit_bytes=24 << 20),
        cost_estimate=pl.CostEstimate(flops=600_000_000, bytes_accessed=6 << 20, transcendentals=8192),
        name="local_states",
    )(k, v, fading, pace)


def chip_kernel(own_ref, other_ref, out_ref, _):
    mine = lax.axis_index(CORE)
    tail = pl.ds(CHIP_COUNT * PIECE, 1)
    own_total, other_total = own_ref[tail, :], other_ref[tail, :]
    later = piece_column(jnp.exp(jnp.where(mine == 0, other_total, own_total)))
    own_factor = jnp.where(mine == 0, later, 1.0)
    other_factor = jnp.where(mine == 0, 1.0, later)
    total = own_total + other_total
    for p in range(CHIP_COUNT):
        at = pl.ds(p * PIECE, PIECE)
        out_ref[pl.ds(p * (PIECE + 1), PIECE), :] = (
            own_factor * own_ref[at, :] + other_factor * other_ref[at, :]
        )
        out_ref[pl.ds(p * (PIECE + 1) + PIECE, 1), :] = total


def chip_states(own, other):
    return pl.pallas_call(
        chip_kernel,
        in_specs=[pl.BlockSpec(memory_space=pltpu.VMEM)] * 2,
        out_specs=[pl.BlockSpec(memory_space=pltpu.VMEM)] * 2,
        out_shape=[
            jax.ShapeDtypeStruct((CHIP_COUNT * (PIECE + 1), 128), F32),
            jax.ShapeDtypeStruct(own.shape, F32),
        ],
        input_output_aliases={0: 1},
        compiler_params=pltpu.CompilerParams(vmem_limit_bytes=8 << 20),
        cost_estimate=pl.CostEstimate(flops=1 << 19, bytes_accessed=3 << 19, transcendentals=128),
        name="chip_states",
    )(own, other)


def scan_kernel(in_ref, out_ref, final_ref, last_ref):
    state = jnp.zeros((PIECE, 128), F32)
    for p in range(CHIP_COUNT):
        out_ref[pl.ds(p * PIECE, PIECE), :] = state
        factor = piece_column(jnp.exp(in_ref[pl.ds(p * (PIECE + 1) + PIECE, 1), :]))
        state = factor * state + in_ref[pl.ds(p * (PIECE + 1), PIECE), :]
    last_ref[...] = state
    for i in range(2):
        final_ref[:, i * 128 : (i + 1) * 128] = last_ref[pl.ds(i, HEADS_HERE, stride=2), :]


def scan_chips(pieces):
    return pl.pallas_call(
        scan_kernel,
        out_shape=[
            jax.ShapeDtypeStruct((CHIP_COUNT * PIECE, 128), F32),
            jax.ShapeDtypeStruct((HEADS_HERE, 2 * HEAD_DIM), F32),
        ],
        scratch_shapes=[pltpu.VMEM((PIECE, 128), F32)],
        compiler_params=pltpu.CompilerParams(vmem_limit_bytes=8 << 20),
        cost_estimate=pl.CostEstimate(flops=1 << 19, bytes_accessed=1 << 20, transcendentals=4096),
        name="scan_chips",
    )(pieces)


def inside_kernel(
    first, q_ref, k_ref, v_ref, fading_ref, pace_ref, even_ref, odd_ref, out_ref, *more
):
    *factor_ref, c_ref, column_ref = more
    g = pl.program_id(0)
    h0 = first + g * GROUP
    second = lax.axis_index(CORE) == 1

    @pl.when(g == 0)
    def _():
        c = log_decay(fading_ref[...], pace_ref[...])
        c_ref[...] = c
        column_ref[...] = to_columns(c)
        if factor_ref:
            partner = jnp.where(second, odd_ref[pl.ds(CHIP_COUNT * PIECE, 1), :], 0.0)
            factor_ref[0][...] = jnp.exp(column_ref[...] + partner)

    columns = pltpu.roll(column_ref[...], lax.rem(128 - h0, 128), axis=1)
    starts = shuffle(
        [
            jnp.stack(
                [
                    jnp.where(second, ref[pl.ds(pl.multiple_of((2 * j + b) * PIECE + 2 * h0, 8), 8), :], 0.0)
                    for j in range(16)
                ]
            )
            for b in range(2)
            for ref in (even_ref, odd_ref)
        ]
    )
    row = lax.broadcasted_iota(jnp.int32, (BLOCK, BLOCK), 0)
    col = lax.broadcasted_iota(jnp.int32, (BLOCK, BLOCK), 1)
    for i in range(GROUP):
        lanes = slice(i * HEAD_DIM, (i + 1) * HEAD_DIM)
        c_row = c_ref[pl.ds(h0 + i, 1), :]
        state = starts[i].reshape(HEAD_DIM, HEAD_DIM)
        base = jnp.zeros((1, 1), F32)
        for b in range(TOKENS_HERE // BLOCK):
            rows = slice(b * BLOCK, (b + 1) * BLOCK)
            q, k, v = q_ref[rows, lanes], k_ref[rows, lanes], v_ref[rows, lanes]
            c_here = c_row[:, rows]
            c_column = columns[rows, i : i + 1]
            diff = c_column - c_here
            factor = jnp.where(row >= col, jnp.exp(jnp.minimum(diff, 0.0)), 0.0)
            weights = (dot(q, k, ((1,), (1,))) * factor).astype(BF16)
            high, low = split(state)
            carried = dot(q, high) + dot(q, low)
            out_ref[rows, lanes] = dot(weights, v) + jnp.exp(c_column - base) * carried
            if b + 1 < TOKENS_HERE // BLOCK:
                last = c_here[:, -1:]
                decayed = k.T.astype(F32) * jnp.exp(last - c_here)
                high, low = split(decayed)
                state = jnp.exp(last - base) * state + dot(high, v) + dot(low, v)
                base = last


def inside(q, k, v, fading, pace, even, odd, first, heads, with_factor):
    at = first // GROUP
    wide = pl.BlockSpec((TOKENS_HERE, GROUP * HEAD_DIM), lambda g: (0, at + g))
    out_specs = [pl.BlockSpec((TOKENS_HERE, GROUP * HEAD_DIM), lambda g: (0, g))]
    out_shape = [jax.ShapeDtypeStruct((TOKENS_HERE, heads * HEAD_DIM), F32)]
    if with_factor:
        out_specs.append(pl.BlockSpec((TOKENS_HERE, 128), lambda g: (0, 0)))
        out_shape.append(jax.ShapeDtypeStruct((TOKENS_HERE, 128), F32))
    return pl.pallas_call(
        functools.partial(inside_kernel, first),
        grid=(heads // GROUP,),
        in_specs=[
            wide,
            wide,
            wide,
            pl.BlockSpec((HEADS_HERE, TOKENS_HERE), lambda g: (0, 0)),
            pl.BlockSpec((1, HEADS_HERE), lambda g: (0, 0)),
            pl.BlockSpec(even.shape, lambda g: (0, 0)),
            pl.BlockSpec(odd.shape, lambda g: (0, 0)),
        ],
        out_specs=out_specs,
        out_shape=out_shape,
        scratch_shapes=[
            pltpu.VMEM((HEADS_HERE, TOKENS_HERE), F32),
            pltpu.VMEM((TOKENS_HERE, 128), F32),
        ],
        compiler_params=pltpu.CompilerParams(vmem_limit_bytes=24 << 20),
        cost_estimate=pl.CostEstimate(
            flops=1_000_000_000, bytes_accessed=6 << 20, transcendentals=1 << 20
        ),
        name="inside",
    )(q, k, v, fading, pace, even, odd)


def outside_kernel(
    q_ref, low_ref, high_ref, own_ref, other_ref, factor_ref, out_ref, squares_ref, sum_ref
):
    g = pl.program_id(0)
    mine = lax.axis_index(CORE)

    @pl.when(g == 0)
    def _():
        sum_ref[...] = jnp.zeros_like(sum_ref)

    columns = pltpu.roll(factor_ref[...], lax.rem(128 - g * GROUP, 128), axis=1)
    own, other = own_ref[...], other_ref[...]
    even = jnp.where(mine == 0, own, other).reshape(16, 2, 8, 128)
    odd = jnp.where(mine == 0, other, own).reshape(16, 2, 8, 128)
    states = shuffle([even[:, 0], odd[:, 0], even[:, 1], odd[:, 1]])
    total = sum_ref[...]
    for i in range(GROUP):
        lanes = slice(i * HEAD_DIM, (i + 1) * HEAD_DIM)
        high, low = split(states[i].reshape(HEAD_DIM, HEAD_DIM))
        q = q_ref[:, lanes]
        carried = dot(jnp.concatenate([q, q], axis=1), jnp.concatenate([high, low], axis=0))
        before = jnp.where(g < GROUPS // 2, low_ref[:, lanes], high_ref[:, lanes])
        out = before + columns[:, i : i + 1] * carried
        out_ref[:, lanes] = out
        total = total + out * out
    sum_ref[...] = total

    @pl.when(g == GROUPS - 1)
    def _():
        squares_ref[...] = jnp.sum(total.T, axis=0, keepdims=True)


def outside(q, before_low, before_high, own, other, factor):
    width = GROUP * HEAD_DIM
    half = GROUPS // 2
    wide = pl.BlockSpec((TOKENS_HERE, width), lambda g: (0, g))
    pieces = pl.BlockSpec((CHIP_COUNT, 8, 128), lambda g: (0, g, 0))
    return pl.pallas_call(
        outside_kernel,
        grid=(GROUPS,),
        in_specs=[
            wide,
            pl.BlockSpec((TOKENS_HERE, width), lambda g: (0, jnp.minimum(g, half - 1))),
            pl.BlockSpec((TOKENS_HERE, width), lambda g: (0, jnp.maximum(g - half, 0))),
            pieces,
            pieces,
            pl.BlockSpec((TOKENS_HERE, 128), lambda g: (0, 0)),
        ],
        out_specs=[wide, pl.BlockSpec((1, TOKENS_HERE), lambda g: (0, 0))],
        out_shape=[
            jax.ShapeDtypeStruct((TOKENS_HERE, HEADS_HERE * HEAD_DIM), F32),
            jax.ShapeDtypeStruct((1, TOKENS_HERE), F32),
        ],
        scratch_shapes=[pltpu.VMEM((TOKENS_HERE, 128), F32)],
        compiler_params=pltpu.CompilerParams(vmem_limit_bytes=24 << 20),
        cost_estimate=pl.CostEstimate(
            flops=600_000_000, bytes_accessed=11 << 20, transcendentals=0
        ),
        name="outside",
    )(q, before_low, before_high, own, other, factor)


def norm_kernel(out_ref, *refs):
    *square_refs, gain_ref, result_ref = refs
    rows = out_ref.shape[0]
    total = sum(ref[...] for ref in square_refs)
    scale = lax.rsqrt(total / D + 1e-06)
    column = jnp.broadcast_to(scale, (128, rows)).T
    for h in range(HEADS_HERE):
        lanes = slice(h * HEAD_DIM, (h + 1) * HEAD_DIM)
        result_ref[:, lanes] = (out_ref[:, lanes] * column * gain_ref[:, lanes]).astype(BF16)


def normed(out, squares, gain):
    rows = 128
    width = HEADS_HERE * HEAD_DIM
    return pl.pallas_call(
        norm_kernel,
        grid=(TOKENS_HERE // rows,),
        in_specs=[
            pl.BlockSpec((rows, width), lambda t: (t, 0)),
            *(pl.BlockSpec((1, rows), lambda t: (0, t)) for _ in squares),
            pl.BlockSpec((1, width), lambda t: (0, 0)),
        ],
        out_specs=pl.BlockSpec((rows, width), lambda t: (t, 0)),
        out_shape=jax.ShapeDtypeStruct((TOKENS_HERE, width), BF16),
        compiler_params=pltpu.CompilerParams(vmem_limit_bytes=24 << 20),
        cost_estimate=pl.CostEstimate(flops=1 << 21, bytes_accessed=6 << 20, transcendentals=512),
        name="normed",
    )(out, *squares, gain)


def turned(value, by):
    count = lax.axis_size("tp")
    return lax.ppermute(value, "tp", [((i + by) % count, i) for i in range(count)])


def layer(q, k, v, pace, fading, gain):
    q, k, v, fading, pace = (
        pltpu.with_memory_space_constraint(part, pltpu.HBM)
        for part in (q, k, v, fading.T, pace.reshape(1, HEADS_HERE))
    )
    keep, send = local_states(k, v, fading, pace)
    swap = [(0, 1), (1, 0)]
    received = lax.ppermute(send, CORE, swap)
    chip, kept = chip_states(keep, received)
    partner = lax.ppermute(kept, CORE, swap)
    gathered = lax.all_to_all(chip.reshape(CHIP_COUNT, PIECE + 1, 1, 128), CHIPS, 0, 0, tiled=True)
    half = HEADS_HERE // 2
    arguments = (q, k, v, fading, pace, partner, received)
    before_low, factor = inside(*arguments, 0, half, True)
    before_low = pltpu.with_memory_space_constraint(before_low, pltpu.HBM)
    prior, final = scan_chips(gathered.reshape(CHIP_COUNT * (PIECE + 1), 128))
    own = lax.all_to_all(prior.reshape(CHIP_COUNT, PIECE, 128), CHIPS, 0, 0, tiled=True)
    (before_high,) = inside(*arguments, half, half, False)
    other = lax.ppermute(own, CORE, swap)
    out, squares = outside(q, before_low, before_high, own, other, factor)
    squares = [squares, *(turned(squares, by) for by in (1, 3, 2))]
    return normed(out, squares, gain.reshape(1, -1)), final


def solution(mesh):
    split_mesh = Mesh(
        mesh.devices.reshape(8, 4, 2, mesh.shape["tp"]), ("seq_0", "seq_1", "seq_2", "tp")
    )
    return jax.shard_map(
        layer,
        mesh=split_mesh,
        in_specs=(P(SEQ, "tp"), P(SEQ, "tp"), P(SEQ, "tp"), P("tp"), P(SEQ, "tp"), P("tp")),
        out_specs=(P(SEQ, "tp"), P("tp", SEQ)),
        check_vma=False,
    )
```

profile of v0, /device:TPU:8, one launch (start us, length us, event | category | flops | bytes accessed | tf_op | source)
XLA Modules:
  0.0 87.2 jit_solution(16694095756162445809)
XLA Ops:
  0.6 4.8 %local_states.1 = (f32[1032,128]{1,0:T(8,128)S(1)}, f32[1032,128]{1,0:T(8,128)S(1)}) custom-call(bf16[512,2048]{1,0:T(8,128)(2,1)} %k_ref.5, bf16[512,2048]{1,0:T(8,128)(2,1)} %v_ref.5, f32[16,512]{1,0:T(8,128)} %bitcast.9, f32[1,16]{1,0:T(1,128)} %bitcast.12), custom_call_target="tpu_custom_call" | custom-call | flops 600000000 | bytes 6291456 | tf_op jit(solution)/shard_map/local_states/pallas_call | solution.py:122
  5.4 0.1 collective-permute-start
  5.5 1.9 %collective-permute-done.other_ref.odd_ref = f32[1032,128]{1,0:T(8,128)S(1)} collective-permute-done((f32[1032,128]{1,0:T(8,128)S(1)}, f32[1032,128]{1,0:T(8,128)S(1)}, u32[]{:S(2)}, u32[]{:S(2)}) %collective-permute-start) | collective-permute-done | bytes 528416 | tf_op jit(solution)/shard_map/ppermute | solution.py:397
  7.4 0.2 chip_states.1
  7.6 29.0 %all_to_all.10 = f32[32,33,1,128]{3,2,1,0:T(1,128)S(1)} all-to-all(f32[32,33,1,128]{3,2,1,0:T(1,128)S(1)} %bitcast.7), channel_id=1, replica_groups=mesh['seq_0'=8,'seq_1'=4,'seq_2'=2,'tp'=4] {'seq_0','seq_1'}, dimensions={0} | all-to-all | bytes 1081344 | tf_op jit(solution)/shard_map/all_to_all | solution.py:400
  36.6 1.0 %scan_chips.1 = (f32[1024,128]{1,0:T(8,128)}, f32[16,256]{1,0:T(8,128)}) custom-call(f32[1056,128]{1,0:T(8,128)S(1)} %bitcast.6), custom_call_target="tpu_custom_call" | custom-call | flops 524288 | bytes 1048576 | tf_op jit(solution)/shard_map/scan_chips/pallas_call | solution.py:190
  37.6 5.6 %all-to-all-start.1 = ((f32[32,32,128]{2,1,0:T(8,128)}), f32[32,32,128]{2,1,0:T(8,128)S(1)}, u32[]{:S(2)}, u32[]{:S(2)}) async-start(f32[32,32,128]{2,1,0:T(8,128)} %bitcast.4), calls=%async_computation.1 | async-start | bytes 1048576 | tf_op jit(solution)/shard_map/all_to_all | solution.py:406
  43.2 0.1 collective-permute-start.1
  43.3 15.9 %all-to-all-done.1.own_ref = f32[32,32,128]{2,1,0:T(8,128)S(1)} async-done(((f32[32,32,128]{2,1,0:T(8,128)}), f32[32,32,128]{2,1,0:T(8,128)S(1)}, u32[]{:S(2)}, u32[]{:S(2)}) %all-to-all-start.1) | async-done | bytes 524320 | tf_op jit(solution)/shard_map/all_to_all | solution.py:406
  59.1 0.0 collective-permute-start.2
  59.1 0.0 collective-permute-done.1.even_ref
  59.1 6.0 %inside.3.high_ref = f32[512,1024]{1,0:T(8,128)S(1)} custom-call(bf16[512,2048]{1,0:T(8,128)(2,1)} %q_ref.5, bf16[512,2048]{1,0:T(8,128)(2,1)} %k_ref.5, bf16[512,2048]{1,0:T(8,128)(2,1)} %v_ref.5, f32[16,512]{1,0:T(8,128)} %bitcast.10, f32[1,16]{1,0:T(1,128)} %bitcast.13, f32[1032,128]{1,0:T(8,128)S(1)} %collective-permute-done.1.even_ref, ...), custom_call_target="tpu_custom_call" | custom-call | flops 1000000000 | bytes 6291456 | tf_op jit(solution)/shard_map/inside/pallas_call | solution.py:267
  65.2 6.0 %inside.2 = (f32[512,1024]{1,0:T(8,128)S(1)}, f32[512,128]{1,0:T(8,128)S(1)}) custom-call(bf16[512,2048]{1,0:T(8,128)(2,1)} %q_ref.5, bf16[512,2048]{1,0:T(8,128)(2,1)} %k_ref.5, bf16[512,2048]{1,0:T(8,128)(2,1)} %v_ref.5, f32[16,512]{1,0:T(8,128)} %bitcast.11, f32[1,16]{1,0:T(1,128)} %bitcast.14, f32[1032,128]{1,0:T(8,128)S(1)} %collective-permute-done.1.even_ref, ...), custom_call_target="tpu_custom_call" | custom-call | flops 1000000000 | bytes 6291456 | tf_op jit(solution)/shard_map/inside/pallas_call | solution.py:267
  71.2 0.0 copy-start
  71.2 1.3 %copy-done = f32[512,1024]{1,0:T(8,128)} copy-done((f32[512,1024]{1,0:T(8,128)}, f32[512,1024]{1,0:T(8,128)S(1)}, u32[]{:S(2)}) %copy-start) | copy-done | bytes 2097176
  72.5 0.0 collective-permute-done.2.other_ref
  72.5 4.6 %outside.1 = (f32[512,2048]{1,0:T(8,128)S(1)}, f32[1,512]{1,0:T(1,128)S(1)}) custom-call(bf16[512,2048]{1,0:T(8,128)(2,1)} %q_ref.5, f32[512,1024]{1,0:T(8,128)} %copy-done, f32[512,1024]{1,0:T(8,128)S(1)} %inside.3.high_ref, f32[32,32,128]{2,1,0:T(8,128)S(1)} %all-to-all-done.1.own_ref, f32[32,32,128]{2,1,0:T(8,128)S(1)} %collective-permute-done.2.other_ref, ...), custom_call_target="tpu_custom_call" | custom-call | flops 600000000 | bytes 11534336 | tf_op jit(solution)/shard_map/outside/pallas_call | solution.py:330
  77.1 3.1 %collective-permute-start.5 = (f32[1,512]{1,0:T(1,128)S(1)}, f32[1,512]{1,0:T(1,128)S(1)}, u32[]{:S(2)}, u32[]{:S(2)}) collective-permute-start(f32[1,512]{1,0:T(1,128)S(1)} %get-tuple-element.20.refs_0_), channel_id=1, source_target_pairs={{2,0},{3,1},{0,2},{1,3},{6,4},{7,5},{4,6},{5,7},{10,8},{11,9},{8,1... | collective-permute-start | bytes 6152 | tf_op jit(solution)/shard_map/ppermute | solution.py:387
  80.2 0.6 collective-permute-start.4
  80.8 2.6 %collective-permute-start.3 = (f32[1,512]{1,0:T(1,128)S(1)}, f32[1,512]{1,0:T(1,128)S(1)}, u32[]{:S(2)}, u32[]{:S(2)}) collective-permute-start(f32[1,512]{1,0:T(1,128)S(1)} %get-tuple-element.20.refs_0_), channel_id=1, source_target_pairs={{1,0},{2,1},{3,2},{0,3},{5,4},{6,5},{7,6},{4,7},{9,8},{10,9},{11,1... | collective-permute-start | bytes 6152 | tf_op jit(solution)/shard_map/ppermute | solution.py:387
  83.4 0.0 collective-permute-done.5.refs_3_
  83.4 1.6 %collective-permute-done.4.refs_2_ = f32[1,512]{1,0:T(1,128)S(1)} collective-permute-done((f32[1,512]{1,0:T(1,128)S(1)}, f32[1,512]{1,0:T(1,128)S(1)}, u32[]{:S(2)}, u32[]{:S(2)}) %collective-permute-start.4) | collective-permute-done | bytes 2080 | tf_op jit(solution)/shard_map/ppermute | solution.py:387
  85.0 0.0 collective-permute-done.3.refs_1_
  85.0 2.2 %normed.1 = bf16[512,2048]{1,0:T(8,128)(2,1)} custom-call(f32[512,2048]{1,0:T(8,128)S(1)} %get-tuple-element.19.out_ref, f32[1,512]{1,0:T(1,128)S(1)} %get-tuple-element.20.refs_0_, f32[1,512]{1,0:T(1,128)S(1)} %collective-permute-done.3.refs_1_, f32[1,512]{1,0:T(1,128)S(1)} %collective-permute-done.4.refs_2_, f32[1,512]{1,0:T(1,128)S(1)} %collective-permute-done.5.refs_3_, ...), custom_call_target="tpu_custom_call" | custom-call | flops 2097152 | bytes 6291456 | tf_op jit(solution)/shard_map/normed/pallas_call | solution.py:369
  (2 shorter events, 0.0 us)
Async XLA Ops:
  5.4 2.0 %collective-permute-start = (f32[1032,128]{1,0:T(8,128)S(1)}, f32[1032,128]{1,0:T(8,128)S(1)}, u32[]{:S(2)}, u32[]{:S(2)}) collective-permute-start(f32[1032,128]{1,0:T(8,128)S(1)} %get-tuple-element.13), channel_id=1, source_target_pairs={{0,4},{4,0},{1,5},{5,1},{2,6},{6,2},{3,7},{7,3},{8,12},{12,8},{9,1... | collective-permute-start | bytes 1585160 | tf_op jit(solution)/shard_map/ppermute | solution.py:397
  37.6 21.5 %all-to-all-start.1 = ((f32[32,32,128]{2,1,0:T(8,128)}), f32[32,32,128]{2,1,0:T(8,128)S(1)}, u32[]{:S(2)}, u32[]{:S(2)}) async-start(f32[32,32,128]{2,1,0:T(8,128)} %bitcast.4), calls=%async_computation.1 | async-start | bytes 1048576 | tf_op jit(solution)/shard_map/all_to_all | solution.py:406
  43.2 16.0 %collective-permute-start.1 = (f32[1032,128]{1,0:T(8,128)S(1)}, f32[1032,128]{1,0:T(8,128)S(1)}, u32[]{:S(2)}, u32[]{:S(2)}) collective-permute-start(f32[1032,128]{1,0:T(8,128)S(1)} %get-tuple-element.14), channel_id=1, source_target_pairs={{0,4},{4,0},{1,5},{5,1},{2,6},{6,2},{3,7},{7,3},{8,12},{12,8},{9,1... | collective-permute-start | bytes 1585160 | tf_op jit(solution)/shard_map/ppermute | solution.py:399
  59.1 13.4 %collective-permute-start.2 = (f32[32,32,128]{2,1,0:T(8,128)S(1)}, f32[32,32,128]{2,1,0:T(8,128)S(1)}, u32[]{:S(2)}, u32[]{:S(2)}) collective-permute-start(f32[32,32,128]{2,1,0:T(8,128)S(1)} %all-to-all-done.1.own_ref), channel_id=1, source_target_pairs={{0,4},{4,0},{1,5},{5,1},{2,6},{6,2},{3,7},{7,3},{8,12},{12,8},{9,1... | collective-permute-start | bytes 1572872 | tf_op jit(solution)/shard_map/ppermute | solution.py:408
  71.2 1.3 %copy-start = (f32[512,1024]{1,0:T(8,128)}, f32[512,1024]{1,0:T(8,128)S(1)}, u32[]{:S(2)}) copy-start(f32[512,1024]{1,0:T(8,128)S(1)} %get-tuple-element.15.low_ref) | copy-start | bytes 6291460
  72.5 12.5 %copy-start.1 = (f32[2048]{0:T(1024)S(1)}, f32[2048]{0:T(1024)}, u32[]{:S(2)}) copy-start(f32[2048]{0:T(1024)} %param.11) | copy-start | bytes 24580
  77.1 6.3 %collective-permute-start.5 = (f32[1,512]{1,0:T(1,128)S(1)}, f32[1,512]{1,0:T(1,128)S(1)}, u32[]{:S(2)}, u32[]{:S(2)}) collective-permute-start(f32[1,512]{1,0:T(1,128)S(1)} %get-tuple-element.20.refs_0_), channel_id=1, source_target_pairs={{2,0},{3,1},{0,2},{1,3},{6,4},{7,5},{4,6},{5,7},{10,8},{11,9},{8,1... | collective-permute-start | bytes 6152 | tf_op jit(solution)/shard_map/ppermute | solution.py:387
  80.2 4.8 %collective-permute-start.4 = (f32[1,512]{1,0:T(1,128)S(1)}, f32[1,512]{1,0:T(1,128)S(1)}, u32[]{:S(2)}, u32[]{:S(2)}) collective-permute-start(f32[1,512]{1,0:T(1,128)S(1)} %get-tuple-element.20.refs_0_), channel_id=1, source_target_pairs={{3,0},{0,1},{1,2},{2,3},{7,4},{4,5},{5,6},{6,7},{11,8},{8,9},{9,10... | collective-permute-start | bytes 6152 | tf_op jit(solution)/shard_map/ppermute | solution.py:387
  80.8 4.2 %collective-permute-start.3 = (f32[1,512]{1,0:T(1,128)S(1)}, f32[1,512]{1,0:T(1,128)S(1)}, u32[]{:S(2)}, u32[]{:S(2)}) collective-permute-start(f32[1,512]{1,0:T(1,128)S(1)} %get-tuple-element.20.refs_0_), channel_id=1, source_target_pairs={{1,0},{2,1},{3,2},{0,3},{5,4},{6,5},{7,6},{4,7},{9,8},{10,9},{11,1... | collective-permute-start | bytes 6152 | tf_op jit(solution)/shard_map/ppermute | solution.py:387
where the time goes:
time: 88.8 us; the launch traced here: 87.2 us
  blocking collectives  29 us (33%)
  Pallas kernels  24.7 us (28%)
  waiting for transfers between devices  19.3 us (22%)
  starting transfers between devices  12.1 us (14%)
  local copies, waits for them, and re-layouts  1.32 us (1%)
    all_to_all x1, blocking collectives, layer(): lax.all_to_all(chip.reshape(CHIP_COUNT, PIECE + 1, 1, 128), CHIPS, 0, 0,...  29 us
    all_to_all x1, waiting for transfers between devices, layer(): lax.all_to_all(prior.reshape(CHIP_COUNT, PIECE, 128), CHIPS, 0, 0, tiled=...  15.9 us
    pallas_call x2, Pallas kernels, inside(): pl.pallas_call(functools.partial(inside_kernel, first), grid=(heads // GR...  12 us
    ppermute x3, starting transfers between devices, turned(): lax.ppermute(value, 'tp', [((i + by) % count, i) for i in range(count)])  6.34 us
    all_to_all x1, starting transfers between devices, layer(): lax.all_to_all(prior.reshape(CHIP_COUNT, PIECE, 128), CHIPS, 0, 0, tiled=...  5.57 us
    pallas_call x1, Pallas kernels, local_states(): pl.pallas_call(state_kernel, grid=(GROUPS,), in_specs=[pl.BlockSpec((TOKE...  4.77 us
    pallas_call x1, Pallas kernels, outside(): pl.pallas_call(outside_kernel, grid=(GROUPS,), in_specs=[wide, pl.BlockSp...  4.55 us
    pallas_call x1, Pallas kernels, normed(): pl.pallas_call(norm_kernel, grid=(TOKENS_HERE // rows,), in_specs=[pl.Blo...  2.21 us
  transfers between devices with their start and end apart: 7, of which 3 were waited for; matrix products, arithmetic and copies ran while one was open for 0% of the time, Pallas kernels for 14%

commit v1 on v0

--- a/solution.py
+++ b/solution.py
@@ -5,15 +5,13 @@
 from jax import lax
 from jax.experimental import pallas as pl
 from jax.experimental.pallas import tpu as pltpu
-from jax.sharding import Mesh
 from jax.sharding import PartitionSpec as P
 
 HEAD_DIM = 128
 BLOCK = 256
 D = 8192
-SEQ = ("seq_0", "seq_1", "seq_2")
-CHIPS = ("seq_0", "seq_1")
-CORE = "seq_2"
+SEQ = "seq"
+SHARDS = 64
 HEADS_HERE = 16
 TOKENS_HERE = 512
 GROUP = 4
@@ -22,6 +20,23 @@
 PIECE = 32
 F32 = jnp.float32
 BF16 = jnp.bfloat16
+
+
+FORTH_REVERSED = True
+BACK_REVERSED = True
+
+
+def core_index():
+    return lax.rem(lax.axis_index(SEQ), 2)
+
+
+def groups(backwards):
+    chips = range(CHIP_COUNT)[::-1] if backwards else range(CHIP_COUNT)
+    return [[2 * chip + core for chip in chips] for core in range(2)]
+
+
+def place(chip, backwards):
+    return CHIP_COUNT - 1 - chip if backwards else chip
 
 
 def dot(a, b, dims=((1,), (0,))):
@@ -85,58 +100,80 @@
     return x
 
 
-def state_kernel(k_ref, v_ref, fading_ref, pace_ref, keep_ref, send_ref, w_ref):
-    g = pl.program_id(0)
-    mine = lax.axis_index(CORE)
-
-    @pl.when(g == 0)
-    def _():
-        c = log_decay(fading_ref[...], pace_ref[...])
-        w_ref[...] = jnp.exp(c[:, -1:] - c)
-        total = jnp.broadcast_to(total_row(c), (8, 128))
-        keep_ref[pl.ds(CHIP_COUNT * PIECE, 8), :] = total
-        send_ref[pl.ds(CHIP_COUNT * PIECE, 8), :] = total
-
-    states = []
-    for i in range(GROUP):
-        lanes = slice(i * HEAD_DIM, (i + 1) * HEAD_DIM)
-        turned = k_ref[:, lanes].T.astype(F32)
-        decayed = turned * w_ref[pl.ds(g * GROUP + i, 1), :]
-        high, low = split(decayed)
-        both = dot(jnp.concatenate([high, low], axis=0), v_ref[:, lanes])
-        state = both[:HEAD_DIM] + both[HEAD_DIM:]
-        states.append(state.reshape(16, 8, 128))
-    units = shuffle(states)
-    for b in range(2):
-        even, odd = units[2 * b], units[2 * b + 1]
-        kept = jnp.where(mine == 0, even, odd)
-        sent = jnp.where(mine == 0, odd, even)
-        for j in range(16):
-            at = pl.ds(pl.multiple_of((2 * j + b) * PIECE + g * 8, 8), 8)
-            keep_ref[at, :] = kept[j]
-            send_ref[at, :] = sent[j]
+def state_kernel(
+    k_hbm, v_hbm, fading_hbm, pace_hbm, keep_ref, send_ref, k_ref, v_ref, fading_ref, pace_ref, w_ref, sems
+):
+    mine = core_index()
+    width = GROUP * HEAD_DIM
+    small = [
+        pltpu.make_async_copy(fading_hbm, fading_ref, sems.at[2 * GROUPS]),
+        pltpu.make_async_copy(pace_hbm, pace_ref, sems.at[2 * GROUPS + 1]),
+    ]
+    for copy in small:
+        copy.start()
+
+    def copies(g):
+        lanes = pl.ds(pl.multiple_of(g * width, width), width)
+        return (
+            pltpu.make_async_copy(k_hbm.at[:, lanes], k_ref.at[g], sems.at[g]),
+            pltpu.make_async_copy(v_hbm.at[:, lanes], v_ref.at[g], sems.at[GROUPS + g]),
+        )
+
+    for g in range(GROUPS):
+        for copy in copies(g):
+            copy.start()
+    for copy in small:
+        copy.wait()
+    c = log_decay(fading_ref[...], pace_ref[...])
+    w_ref[...] = jnp.exp(c[:, -1:] - c)
+    total = jnp.broadcast_to(total_row(c), (8, 128))
+    keep_ref[pl.ds(CHIP_COUNT * PIECE, 8), :] = total
+    send_ref[pl.ds(CHIP_COUNT * PIECE, 8), :] = total
+
+    def group(g, carry):
+        for copy in copies(g):
+            copy.wait()
+        states = []
+        for i in range(GROUP):
+            lanes = slice(i * HEAD_DIM, (i + 1) * HEAD_DIM)
+            turned = k_ref[g, :, lanes].T.astype(F32)
+            decayed = turned * w_ref[pl.ds(g * GROUP + i, 1), :]
+            high, low = split(decayed)
+            both = dot(jnp.concatenate([high, low], axis=0), v_ref[g, :, lanes])
+            state = both[:HEAD_DIM] + both[HEAD_DIM:]
+            states.append(state.reshape(16, 8, 128))
+        units = shuffle(states)
+        for b in range(2):
+            even, odd = units[2 * b], units[2 * b + 1]
+            kept = jnp.where(mine == 0, even, odd)
+            sent = jnp.where(mine == 0, odd, even)
+            for j in range(16):
+                at = pl.ds(pl.multiple_of((2 * j + b) * PIECE + g * 8, 8), 8)
+                keep_ref[at, :] = kept[j]
+                send_ref[at, :] = sent[j]
+        return carry
+
+    lax.fori_loop(0, GROUPS, group, 0)
 
 
 def local_states(k, v, fading, pace):
     rows = CHIP_COUNT * PIECE + 8
     return pl.pallas_call(
         state_kernel,
-        grid=(GROUPS,),
-        in_specs=[
-            pl.BlockSpec((TOKENS_HERE, GROUP * HEAD_DIM), lambda g: (0, g)),
-            pl.BlockSpec((TOKENS_HERE, GROUP * HEAD_DIM), lambda g: (0, g)),
-            pl.BlockSpec((HEADS_HERE, TOKENS_HERE), lambda g: (0, 0)),
-            pl.BlockSpec((1, HEADS_HERE), lambda g: (0, 0)),
-        ],
-        out_specs=[
-            pl.BlockSpec((rows, 128), lambda g: (0, 0)),
-            pl.BlockSpec((rows, 128), lambda g: (0, 0)),
-        ],
+        in_specs=[pl.BlockSpec(memory_space=pl.ANY)] * 4,
+        out_specs=[pl.BlockSpec(memory_space=pltpu.VMEM)] * 2,
         out_shape=[
             jax.ShapeDtypeStruct((rows, 128), F32),
             jax.ShapeDtypeStruct((rows, 128), F32),
         ],
-        scratch_shapes=[pltpu.VMEM((HEADS_HERE, TOKENS_HERE), F32)],
+        scratch_shapes=[
+            pltpu.VMEM((GROUPS, TOKENS_HERE, GROUP * HEAD_DIM), BF16),
+            pltpu.VMEM((GROUPS, TOKENS_HERE, GROUP * HEAD_DIM), BF16),
+            pltpu.VMEM((HEADS_HERE, TOKENS_HERE), F32),
+            pltpu.VMEM((1, HEADS_HERE), F32),
+            pltpu.VMEM((HEADS_HERE, TOKENS_HERE), F32),
+            pltpu.SemaphoreType.DMA((2 * GROUPS + 2,)),
+        ],
         compiler_params=pltpu.CompilerParams(vmem_limit_bytes=24 << 20),
         cost_estimate=pl.CostEstimate(flops=600_000_000, bytes_accessed=6 << 20, transcendentals=8192),
         name="local_states",
@@ -144,7 +181,7 @@
 
 
 def chip_kernel(own_ref, other_ref, out_ref, _):
-    mine = lax.axis_index(CORE)
+    mine = core_index()
     tail = pl.ds(CHIP_COUNT * PIECE, 1)
     own_total, other_total = own_ref[tail, :], other_ref[tail, :]
     later = piece_column(jnp.exp(jnp.where(mine == 0, other_total, own_total)))
@@ -153,10 +190,11 @@
     total = own_total + other_total
     for p in range(CHIP_COUNT):
         at = pl.ds(p * PIECE, PIECE)
-        out_ref[pl.ds(p * (PIECE + 1), PIECE), :] = (
+        to = place(p, FORTH_REVERSED) * (PIECE + 1)
+        out_ref[pl.ds(to, PIECE), :] = (
             own_factor * own_ref[at, :] + other_factor * other_ref[at, :]
         )
-        out_ref[pl.ds(p * (PIECE + 1) + PIECE, 1), :] = total
+        out_ref[pl.ds(to + PIECE, 1), :] = total
 
 
 def chip_states(own, other):
@@ -178,9 +216,10 @@
 def scan_kernel(in_ref, out_ref, final_ref, last_ref):
     state = jnp.zeros((PIECE, 128), F32)
     for p in range(CHIP_COUNT):
-        out_ref[pl.ds(p * PIECE, PIECE), :] = state
-        factor = piece_column(jnp.exp(in_ref[pl.ds(p * (PIECE + 1) + PIECE, 1), :]))
-        state = factor * state + in_ref[pl.ds(p * (PIECE + 1), PIECE), :]
+        out_ref[pl.ds(place(p, BACK_REVERSED) * PIECE, PIECE), :] = state
+        at = place(p, FORTH_REVERSED) * (PIECE + 1)
+        factor = piece_column(jnp.exp(in_ref[pl.ds(at + PIECE, 1), :]))
+        state = factor * state + in_ref[pl.ds(at, PIECE), :]
     last_ref[...] = state
     for i in range(2):
         final_ref[:, i * 128 : (i + 1) * 128] = last_ref[pl.ds(i, HEADS_HERE, stride=2), :]
@@ -206,7 +245,7 @@
     *factor_ref, c_ref, column_ref = more
     g = pl.program_id(0)
     h0 = first + g * GROUP
-    second = lax.axis_index(CORE) == 1
+    second = core_index() == 1
 
     @pl.when(g == 0)
     def _():
@@ -291,91 +330,140 @@
 
 
 def outside_kernel(
-    q_ref, low_ref, high_ref, own_ref, other_ref, factor_ref, out_ref, squares_ref, sum_ref
+    q_hbm, low_hbm, own_hbm, high_ref, other_ref, factor_ref, out_ref, squares_ref, q_ref, low_ref, own_ref, sum_ref, sems
 ):
-    g = pl.program_id(0)
-    mine = lax.axis_index(CORE)
-
-    @pl.when(g == 0)
-    def _():
-        sum_ref[...] = jnp.zeros_like(sum_ref)
-
-    columns = pltpu.roll(factor_ref[...], lax.rem(128 - g * GROUP, 128), axis=1)
-    own, other = own_ref[...], other_ref[...]
-    even = jnp.where(mine == 0, own, other).reshape(16, 2, 8, 128)
-    odd = jnp.where(mine == 0, other, own).reshape(16, 2, 8, 128)
-    states = shuffle([even[:, 0], odd[:, 0], even[:, 1], odd[:, 1]])
-    total = sum_ref[...]
-    for i in range(GROUP):
-        lanes = slice(i * HEAD_DIM, (i + 1) * HEAD_DIM)
-        high, low = split(states[i].reshape(HEAD_DIM, HEAD_DIM))
-        q = q_ref[:, lanes]
-        carried = dot(jnp.concatenate([q, q], axis=1), jnp.concatenate([high, low], axis=0))
-        before = jnp.where(g < GROUPS // 2, low_ref[:, lanes], high_ref[:, lanes])
-        out = before + columns[:, i : i + 1] * carried
-        out_ref[:, lanes] = out
-        total = total + out * out
-    sum_ref[...] = total
-
-    @pl.when(g == GROUPS - 1)
-    def _():
-        squares_ref[...] = jnp.sum(total.T, axis=0, keepdims=True)
+    mine = core_index()
+    width = GROUP * HEAD_DIM
+    half = GROUPS // 2
+    own_copy = pltpu.make_async_copy(own_hbm, own_ref, sems.at[2 * GROUPS])
+    own_copy.start()
+
+    def copies(g, low):
+        lanes = pl.ds(pl.multiple_of(g * width, width), width)
+        found = [pltpu.make_async_copy(q_hbm.at[:, lanes], q_ref.at[g], sems.at[g])]
+        if low:
+            found.append(pltpu.make_async_copy(low_hbm.at[:, lanes], low_ref.at[g], sems.at[GROUPS + g]))
+        return found
+
+    for g in range(GROUPS):
+        for copy in copies(g, g < half):
+            copy.start()
+    own_copy.wait()
+
+    def group(g, low):
+        for copy in copies(g, low):
+            copy.wait()
+        columns = pltpu.roll(factor_ref[...], lax.rem(128 - g * GROUP, 128), axis=1)
+        rows = pl.ds(pl.multiple_of(g * 8, 8), 8)
+        own, other = (
+            jnp.stack([ref[place(p, BACK_REVERSED), rows, :] for p in range(CHIP_COUNT)])
+            for ref in (own_ref, other_ref)
+        )
+        even = jnp.where(mine == 0, own, other).reshape(16, 2, 8, 128)
+        odd = jnp.where(mine == 0, other, own).reshape(16, 2, 8, 128)
+        states = shuffle([even[:, 0], odd[:, 0], even[:, 1], odd[:, 1]])
+        start = g * width if low else (g - half) * width
+        total = None
+        for i in range(GROUP):
+            lanes = slice(i * HEAD_DIM, (i + 1) * HEAD_DIM)
+            high, low_part = split(states[i].reshape(HEAD_DIM, HEAD_DIM))
+            q = q_ref[g, :, lanes]
+            carried = dot(jnp.concatenate([q, q], axis=1), jnp.concatenate([high, low_part], axis=0))
+            if low:
+                before = low_ref[g, :, lanes]
+            else:
+                before = high_ref[:, pl.ds(pl.multiple_of(start + i * HEAD_DIM, HEAD_DIM), HEAD_DIM)]
+            out = before + columns[:, i : i + 1] * carried
+            out_ref[:, pl.ds(pl.multiple_of(g * width + i * HEAD_DIM, HEAD_DIM), HEAD_DIM)] = out
+            total = out * out if total is None else total + out * out
+        return total
+
+    sum_ref[...] = jnp.zeros_like(sum_ref)
+
+    def low_group(g, carry):
+        sum_ref[...] += group(g, True)
+        return carry
+
+    def high_group(g, carry):
+        sum_ref[...] += group(g, False)
+        return carry
+
+    lax.fori_loop(0, half, low_group, 0)
+    lax.fori_loop(half, GROUPS, high_group, 0)
+    squares_ref[...] = jnp.sum(sum_ref[...].T, axis=0, keepdims=True)
 
 
 def outside(q, before_low, before_high, own, other, factor):
     width = GROUP * HEAD_DIM
     half = GROUPS // 2
-    wide = pl.BlockSpec((TOKENS_HERE, width), lambda g: (0, g))
-    pieces = pl.BlockSpec((CHIP_COUNT, 8, 128), lambda g: (0, g, 0))
+    here = pl.BlockSpec(memory_space=pltpu.VMEM)
     return pl.pallas_call(
         outside_kernel,
-        grid=(GROUPS,),
-        in_specs=[
-            wide,
-            pl.BlockSpec((TOKENS_HERE, width), lambda g: (0, jnp.minimum(g, half - 1))),
-            pl.BlockSpec((TOKENS_HERE, width), lambda g: (0, jnp.maximum(g - half, 0))),
-            pieces,
-            pieces,
-            pl.BlockSpec((TOKENS_HERE, 128), lambda g: (0, 0)),
-        ],
-        out_specs=[wide, pl.BlockSpec((1, TOKENS_HERE), lambda g: (0, 0))],
+        in_specs=[pl.BlockSpec(memory_space=pl.ANY)] * 3 + [here] * 3,
+        out_specs=[here, here],
         out_shape=[
             jax.ShapeDtypeStruct((TOKENS_HERE, HEADS_HERE * HEAD_DIM), F32),
             jax.ShapeDtypeStruct((1, TOKENS_HERE), F32),
         ],
-        scratch_shapes=[pltpu.VMEM((TOKENS_HERE, 128), F32)],
+        scratch_shapes=[
+            pltpu.VMEM((GROUPS, TOKENS_HERE, width), BF16),
+            pltpu.VMEM((half, TOKENS_HERE, width), F32),
+            pltpu.VMEM(own.shape, F32),
+            pltpu.VMEM((TOKENS_HERE, 128), F32),
+            pltpu.SemaphoreType.DMA((2 * GROUPS + 1,)),
+        ],
         compiler_params=pltpu.CompilerParams(vmem_limit_bytes=24 << 20),
         cost_estimate=pl.CostEstimate(
             flops=600_000_000, bytes_accessed=11 << 20, transcendentals=0
         ),
         name="outside",
-    )(q, before_low, before_high, own, other, factor)
+    )(q, before_low, own, before_high, other, factor)
+
+
+NORM_ROWS = 64
 
 
 def norm_kernel(out_ref, *refs):
-    *square_refs, gain_ref, result_ref = refs
-    rows = out_ref.shape[0]
+    *square_refs, gain_ref, result_hbm, column_ref, result_ref, sems = refs
     total = sum(ref[...] for ref in square_refs)
     scale = lax.rsqrt(total / D + 1e-06)
-    column = jnp.broadcast_to(scale, (128, rows)).T
-    for h in range(HEADS_HERE):
-        lanes = slice(h * HEAD_DIM, (h + 1) * HEAD_DIM)
-        result_ref[:, lanes] = (out_ref[:, lanes] * column * gain_ref[:, lanes]).astype(BF16)
+    column_ref[...] = jnp.broadcast_to(scale, (128, TOKENS_HERE)).T
+    steps = TOKENS_HERE // NORM_ROWS
+
+    def write(t):
+        rows = pl.ds(pl.multiple_of(t * NORM_ROWS, NORM_ROWS), NORM_ROWS)
+        return pltpu.make_async_copy(result_ref.at[rows, :], result_hbm.at[rows, :], sems.at[t])
+
+    def step(t, carry):
+        rows = pl.ds(pl.multiple_of(t * NORM_ROWS, NORM_ROWS), NORM_ROWS)
+        column = column_ref[rows, :]
+        for h in range(HEADS_HERE):
+            lanes = slice(h * HEAD_DIM, (h + 1) * HEAD_DIM)
+            result_ref[rows, lanes] = (out_ref[rows, lanes] * column * gain_ref[:, lanes]).astype(BF16)
+        write(t).start()
+        return carry
+
+    def finish(t, carry):
+        write(t).wait()
+        return carry
+
+    lax.fori_loop(0, steps, step, 0)
+    lax.fori_loop(0, steps, finish, 0)
 
 
 def normed(out, squares, gain):
-    rows = 128
     width = HEADS_HERE * HEAD_DIM
+    here = pl.BlockSpec(memory_space=pltpu.VMEM)
     return pl.pallas_call(
         norm_kernel,
-        grid=(TOKENS_HERE // rows,),
-        in_specs=[
-            pl.BlockSpec((rows, width), lambda t: (t, 0)),
-            *(pl.BlockSpec((1, rows), lambda t: (0, t)) for _ in squares),
-            pl.BlockSpec((1, width), lambda t: (0, 0)),
-        ],
-        out_specs=pl.BlockSpec((rows, width), lambda t: (t, 0)),
+        in_specs=[here] * (2 + len(squares)),
+        out_specs=pl.BlockSpec(memory_space=pl.ANY),
         out_shape=jax.ShapeDtypeStruct((TOKENS_HERE, width), BF16),
+        scratch_shapes=[
+            pltpu.VMEM((TOKENS_HERE, 128), F32),
+            pltpu.VMEM((TOKENS_HERE, width), BF16),
+            pltpu.SemaphoreType.DMA((TOKENS_HERE // NORM_ROWS,)),
+        ],
         compiler_params=pltpu.CompilerParams(vmem_limit_bytes=24 << 20),
         cost_estimate=pl.CostEstimate(flops=1 << 21, bytes_accessed=6 << 20, transcendentals=512),
         name="normed",
@@ -393,31 +481,42 @@
         for part in (q, k, v, fading.T, pace.reshape(1, HEADS_HERE))
     )
     keep, send = local_states(k, v, fading, pace)
-    swap = [(0, 1), (1, 0)]
-    received = lax.ppermute(send, CORE, swap)
+    swap = [(i, i ^ 1) for i in range(SHARDS)]
+    received = lax.ppermute(send, SEQ, swap)
     chip, kept = chip_states(keep, received)
-    partner = lax.ppermute(kept, CORE, swap)
-    gathered = lax.all_to_all(chip.reshape(CHIP_COUNT, PIECE + 1, 1, 128), CHIPS, 0, 0, tiled=True)
+    partner = lax.ppermute(kept, SEQ, swap)
+    gathered = lax.all_to_all(
+        chip.reshape(CHIP_COUNT, PIECE + 1, 1, 128),
+        SEQ,
+        0,
+        0,
+        axis_index_groups=groups(FORTH_REVERSED),
+        tiled=True,
+    )
     half = HEADS_HERE // 2
     arguments = (q, k, v, fading, pace, partner, received)
     before_low, factor = inside(*arguments, 0, half, True)
     before_low = pltpu.with_memory_space_constraint(before_low, pltpu.HBM)
     prior, final = scan_chips(gathered.reshape(CHIP_COUNT * (PIECE + 1), 128))
-    own = lax.all_to_all(prior.reshape(CHIP_COUNT, PIECE, 128), CHIPS, 0, 0, tiled=True)
+    own = lax.all_to_all(
+        prior.reshape(CHIP_COUNT, PIECE, 128),
+        SEQ,
+        0,
+        0,
+        axis_index_groups=groups(BACK_REVERSED),
+        tiled=True,
+    )
     (before_high,) = inside(*arguments, half, half, False)
-    other = lax.ppermute(own, CORE, swap)
+    other = lax.ppermute(own, SEQ, swap)
     out, squares = outside(q, before_low, before_high, own, other, factor)
     squares = [squares, *(turned(squares, by) for by in (1, 3, 2))]
     return normed(out, squares, gain.reshape(1, -1)), final
 
 
 def solution(mesh):
-    split_mesh = Mesh(
-        mesh.devices.reshape(8, 4, 2, mesh.shape["tp"]), ("seq_0", "seq_1", "seq_2", "tp")
-    )
     return jax.shard_map(
         layer,
-        mesh=split_mesh,
+        mesh=mesh,
         in_specs=(P(SEQ, "tp"), P(SEQ, "tp"), P(SEQ, "tp"), P("tp"), P(SEQ, "tp"), P("tp")),
         out_specs=(P(SEQ, "tp"), P("tp", SEQ)),
         check_vma=False,

time: 88.8 us -> 83 us (0.935)
  the two profiles are of different devices: /device:TPU:8 before, /device:TPU:6 now
where the time goes in v1:
time: 83 us; the launch traced here: 82.7 us
  blocking collectives  26.5 us (32%)
  Pallas kernels  22.4 us (27%)
  waiting for transfers between devices  19.2 us (23%)
  starting transfers between devices  12.5 us (15%)
  local copies, waits for them, and re-layouts  1.32 us (2%)
    all_to_all x1, blocking collectives, layer(): lax.all_to_all(chip.reshape(CHIP_COUNT, PIECE + 1, 1, 128), SEQ, 0, 0, ax...  26.5 us
    all_to_all x1, waiting for transfers between devices, layer(): lax.all_to_all(prior.reshape(CHIP_COUNT, PIECE, 128), SEQ, 0, 0, axis_ind...  12.5 us
    pallas_call x2, Pallas kernels, inside(): pl.pallas_call(functools.partial(inside_kernel, first), grid=(heads // GR...  12 us
    all_to_all x1, starting transfers between devices, layer(): lax.all_to_all(prior.reshape(CHIP_COUNT, PIECE, 128), SEQ, 0, 0, axis_ind...  8.74 us
    ppermute x3, waiting for transfers between devices, turned(): lax.ppermute(value, 'tp', [((i + by) % count, i) for i in range(count)])  4.79 us
    pallas_call x1, Pallas kernels, outside(): pl.pallas_call(outside_kernel, in_specs=[pl.BlockSpec(memory_space=pl.ANY...  4.05 us
    ppermute x3, starting transfers between devices, turned(): lax.ppermute(value, 'tp', [((i + by) % count, i) for i in range(count)])  3.59 us
    pallas_call x1, Pallas kernels, local_states(): pl.pallas_call(state_kernel, in_specs=[pl.BlockSpec(memory_space=pl.ANY)]...  3.55 us
  transfers between devices with their start and end apart: 7, of which 4 were waited for; matrix products, arithmetic and copies ran while one was open for 0% of the time, Pallas kernels for 15%

profile of v1, /device:TPU:6, one launch (start us, length us, event | category | flops | bytes accessed | tf_op | source)
XLA Modules:
  0.0 82.7 jit_solution(6183928938784443188)
XLA Ops:
  0.6 3.6 %local_states.1 = (f32[1032,128]{1,0:T(8,128)S(1)}, f32[1032,128]{1,0:T(8,128)S(1)}) custom-call(bf16[512,2048]{1,0:T(8,128)(2,1)} %k_ref.3, bf16[512,2048]{1,0:T(8,128)(2,1)} %v_ref.3, f32[16,512]{1,0:T(8,128)} %bitcast.9, f32[1,16]{1,0:T(1,128)} %bitcast.12), custom_call_target="tpu_custom_call" | custom-call | flops 600000000 | bytes 6291456 | tf_op jit(solution)/shard_map/local_states/pallas_call | solution.py:161
  4.2 0.1 collective-permute-start
  4.3 1.9 %collective-permute-done.other_ref.odd_ref = f32[1032,128]{1,0:T(8,128)S(1)} collective-permute-done((f32[1032,128]{1,0:T(8,128)S(1)}, f32[1032,128]{1,0:T(8,128)S(1)}, u32[]{:S(2)}, u32[]{:S(2)}) %collective-permute-start) | collective-permute-done | bytes 528416 | tf_op jit(solution)/shard_map/ppermute | solution.py:485
  6.2 0.2 chip_states.1
  6.4 26.5 %all_to_all.10 = f32[32,33,1,128]{3,2,1,0:T(1,128)S(1)} all-to-all(f32[32,33,1,128]{3,2,1,0:T(1,128)S(1)} %bitcast.7), channel_id=1, replica_groups={{248,240,232,224,216,208,200,192,184,176,168,160,152,144,136,128,120,11..., dimensions={0} | all-to-all | bytes 1081344 | tf_op jit(solution)/shard_map/all_to_all | solution.py:488
  32.9 1.0 %scan_chips.1 = (f32[1024,128]{1,0:T(8,128)}, f32[16,256]{1,0:T(8,128)}) custom-call(f32[1056,128]{1,0:T(8,128)S(1)} %bitcast.6), custom_call_target="tpu_custom_call" | custom-call | flops 524288 | bytes 1048576 | tf_op jit(solution)/shard_map/scan_chips/pallas_call | solution.py:229
  33.9 8.7 %all-to-all-start.1 = ((f32[32,32,128]{2,1,0:T(8,128)}), f32[32,32,128]{2,1,0:T(8,128)S(1)}, u32[]{:S(2)}, u32[]{:S(2)}) async-start(f32[32,32,128]{2,1,0:T(8,128)} %bitcast.4), calls=%async_computation.1 | async-start | bytes 1048576 | tf_op jit(solution)/shard_map/all_to_all | solution.py:501
  42.6 0.1 collective-permute-start.1
  42.7 12.5 %all-to-all-done.1.own_hbm = f32[32,32,128]{2,1,0:T(8,128)S(1)} async-done(((f32[32,32,128]{2,1,0:T(8,128)}), f32[32,32,128]{2,1,0:T(8,128)S(1)}, u32[]{:S(2)}, u32[]{:S(2)}) %all-to-all-start.1) | async-done | bytes 524320 | tf_op jit(solution)/shard_map/all_to_all | solution.py:501
  55.3 0.0 collective-permute-start.2
  55.3 0.0 collective-permute-done.1.even_ref
  55.3 6.0 %inside.3.high_ref = f32[512,1024]{1,0:T(8,128)S(1)} custom-call(bf16[512,2048]{1,0:T(8,128)(2,1)} %q_hbm.1, bf16[512,2048]{1,0:T(8,128)(2,1)} %k_ref.3, bf16[512,2048]{1,0:T(8,128)(2,1)} %v_ref.3, f32[16,512]{1,0:T(8,128)} %bitcast.10, f32[1,16]{1,0:T(1,128)} %bitcast.13, f32[1032,128]{1,0:T(8,128)S(1)} %collective-permute-done.1.even_ref, ...), custom_call_target="tpu_custom_call" | custom-call | flops 1000000000 | bytes 6291456 | tf_op jit(solution)/shard_map/inside/pallas_call | solution.py:306
  61.3 6.0 %inside.2 = (f32[512,1024]{1,0:T(8,128)S(1)}, f32[512,128]{1,0:T(8,128)S(1)}) custom-call(bf16[512,2048]{1,0:T(8,128)(2,1)} %q_hbm.1, bf16[512,2048]{1,0:T(8,128)(2,1)} %k_ref.3, bf16[512,2048]{1,0:T(8,128)(2,1)} %v_ref.3, f32[16,512]{1,0:T(8,128)} %bitcast.11, f32[1,16]{1,0:T(1,128)} %bitcast.14, f32[1032,128]{1,0:T(8,128)S(1)} %collective-permute-done.1.even_ref, ...), custom_call_target="tpu_custom_call" | custom-call | flops 1000000000 | bytes 6291456 | tf_op jit(solution)/shard_map/inside/pallas_call | solution.py:306
  67.4 0.0 copy-start
  67.4 1.3 %copy-done = f32[512,1024]{1,0:T(8,128)} copy-done((f32[512,1024]{1,0:T(8,128)}, f32[512,1024]{1,0:T(8,128)S(1)}, u32[]{:S(2)}) %copy-start) | copy-done | bytes 2097176
  68.7 0.0 collective-permute-done.2.other_ref
  68.7 4.0 %outside.1 = (f32[512,2048]{1,0:T(8,128)S(1)}, f32[1,512]{1,0:T(1,128)S(1)}) custom-call(bf16[512,2048]{1,0:T(8,128)(2,1)} %q_hbm.1, f32[512,1024]{1,0:T(8,128)} %copy-done, f32[32,32,128]{2,1,0:T(8,128)S(1)} %all-to-all-done.1.own_hbm, f32[512,1024]{1,0:T(8,128)S(1)} %inside.3.high_ref, f32[32,32,128]{2,1,0:T(8,128)S(1)} %collective-permute-done.2.other_ref, ...), custom_call_target="tpu_custom_call" | custom-call | flops 600000000 | bytes 11534336 | tf_op jit(solution)/shard_map/outside/pallas_call | solution.py:400
  72.7 1.5 %collective-permute-start.5 = (f32[1,512]{1,0:T(1,128)S(1)}, f32[1,512]{1,0:T(1,128)S(1)}, u32[]{:S(2)}, u32[]{:S(2)}) collective-permute-start(f32[1,512]{1,0:T(1,128)S(1)} %get-tuple-element.20.refs_0_), channel_id=1, source_target_pairs={{2,0},{3,1},{0,2},{1,3},{6,4},{7,5},{4,6},{5,7},{10,8},{11,9},{8,1... | collective-permute-start | bytes 6152 | tf_op jit(solution)/shard_map/ppermute | solution.py:475
  74.2 2.1 %collective-permute-start.4 = (f32[1,512]{1,0:T(1,128)S(1)}, f32[1,512]{1,0:T(1,128)S(1)}, u32[]{:S(2)}, u32[]{:S(2)}) collective-permute-start(f32[1,512]{1,0:T(1,128)S(1)} %get-tuple-element.20.refs_0_), channel_id=1, source_target_pairs={{3,0},{0,1},{1,2},{2,3},{7,4},{4,5},{5,6},{6,7},{11,8},{8,9},{9,10... | collective-permute-start | bytes 6152 | tf_op jit(solution)/shard_map/ppermute | solution.py:475
  76.3 0.0 collective-permute-start.3
  76.3 1.6 %collective-permute-done.5.refs_3_ = f32[1,512]{1,0:T(1,128)S(1)} collective-permute-done((f32[1,512]{1,0:T(1,128)S(1)}, f32[1,512]{1,0:T(1,128)S(1)}, u32[]{:S(2)}, u32[]{:S(2)}) %collective-permute-start.5) | collective-permute-done | bytes 2080 | tf_op jit(solution)/shard_map/ppermute | solution.py:475
  77.9 0.0 collective-permute-done.4.refs_2_
  77.9 3.2 %collective-permute-done.3.refs_1_ = f32[1,512]{1,0:T(1,128)S(1)} collective-permute-done((f32[1,512]{1,0:T(1,128)S(1)}, f32[1,512]{1,0:T(1,128)S(1)}, u32[]{:S(2)}, u32[]{:S(2)}) %collective-permute-start.3) | collective-permute-done | bytes 2080 | tf_op jit(solution)/shard_map/ppermute | solution.py:475
  81.1 1.6 %normed.1 = bf16[512,2048]{1,0:T(8,128)(2,1)} custom-call(f32[512,2048]{1,0:T(8,128)S(1)} %get-tuple-element.19.out_ref, f32[1,512]{1,0:T(1,128)S(1)} %get-tuple-element.20.refs_0_, f32[1,512]{1,0:T(1,128)S(1)} %collective-permute-done.3.refs_1_, f32[1,512]{1,0:T(1,128)S(1)} %collective-permute-done.4.refs_2_, f32[1,512]{1,0:T(1,128)S(1)} %collective-permute-done.5.refs_3_, ...), custom_call_target="tpu_custom_call" | custom-call | flops 2097152 | bytes 6291456 | tf_op jit(solution)/shard_map/normed/pallas_call | solution.py:457
  (2 shorter events, 0.0 us)
Async XLA Ops:
  4.2 2.0 %collective-permute-start = (f32[1032,128]{1,0:T(8,128)S(1)}, f32[1032,128]{1,0:T(8,128)S(1)}, u32[]{:S(2)}, u32[]{:S(2)}) collective-permute-start(f32[1032,128]{1,0:T(8,128)S(1)} %get-tuple-element.13), channel_id=1, source_target_pairs={{0,4},{4,0},{8,12},{12,8},{16,20},{20,16},{24,28},{28,24},{32,36},... | collective-permute-start | bytes 1585160 | tf_op jit(solution)/shard_map/ppermute | solution.py:485
  33.9 21.4 %all-to-all-start.1 = ((f32[32,32,128]{2,1,0:T(8,128)}), f32[32,32,128]{2,1,0:T(8,128)S(1)}, u32[]{:S(2)}, u32[]{:S(2)}) async-start(f32[32,32,128]{2,1,0:T(8,128)} %bitcast.4), calls=%async_computation.1 | async-start | bytes 1048576 | tf_op jit(solution)/shard_map/all_to_all | solution.py:501
  42.6 12.7 %collective-permute-start.1 = (f32[1032,128]{1,0:T(8,128)S(1)}, f32[1032,128]{1,0:T(8,128)S(1)}, u32[]{:S(2)}, u32[]{:S(2)}) collective-permute-start(f32[1032,128]{1,0:T(8,128)S(1)} %get-tuple-element.14), channel_id=1, source_target_pairs={{0,4},{4,0},{8,12},{12,8},{16,20},{20,16},{24,28},{28,24},{32,36},... | collective-permute-start | bytes 1585160 | tf_op jit(solution)/shard_map/ppermute | solution.py:487
  55.3 13.4 %collective-permute-start.2 = (f32[32,32,128]{2,1,0:T(8,128)S(1)}, f32[32,32,128]{2,1,0:T(8,128)S(1)}, u32[]{:S(2)}, u32[]{:S(2)}) collective-permute-start(f32[32,32,128]{2,1,0:T(8,128)S(1)} %all-to-all-done.1.own_hbm), channel_id=1, source_target_pairs={{0,4},{4,0},{8,12},{12,8},{16,20},{20,16},{24,28},{28,24},{32,36},... | collective-permute-start | bytes 1572872 | tf_op jit(solution)/shard_map/ppermute | solution.py:510
  67.4 1.3 %copy-start = (f32[512,1024]{1,0:T(8,128)}, f32[512,1024]{1,0:T(8,128)S(1)}, u32[]{:S(2)}) copy-start(f32[512,1024]{1,0:T(8,128)S(1)} %get-tuple-element.15.low_hbm) | copy-start | bytes 6291460
  68.7 12.4 %copy-start.1 = (f32[2048]{0:T(1024)S(1)}, f32[2048]{0:T(1024)}, u32[]{:S(2)}) copy-start(f32[2048]{0:T(1024)} %param.11) | copy-start | bytes 24580
  72.7 5.2 %collective-permute-start.5 = (f32[1,512]{1,0:T(1,128)S(1)}, f32[1,512]{1,0:T(1,128)S(1)}, u32[]{:S(2)}, u32[]{:S(2)}) collective-permute-start(f32[1,512]{1,0:T(1,128)S(1)} %get-tuple-element.20.refs_0_), channel_id=1, source_target_pairs={{2,0},{3,1},{0,2},{1,3},{6,4},{7,5},{4,6},{5,7},{10,8},{11,9},{8,1... | collective-permute-start | bytes 6152 | tf_op jit(solution)/shard_map/ppermute | solution.py:475
  74.2 3.7 %collective-permute-start.4 = (f32[1,512]{1,0:T(1,128)S(1)}, f32[1,512]{1,0:T(1,128)S(1)}, u32[]{:S(2)}, u32[]{:S(2)}) collective-permute-start(f32[1,512]{1,0:T(1,128)S(1)} %get-tuple-element.20.refs_0_), channel_id=1, source_target_pairs={{3,0},{0,1},{1,2},{2,3},{7,4},{4,5},{5,6},{6,7},{11,8},{8,9},{9,10... | collective-permute-start | bytes 6152 | tf_op jit(solution)/shard_map/ppermute | solution.py:475
  76.3 4.8 %collective-permute-start.3 = (f32[1,512]{1,0:T(1,128)S(1)}, f32[1,512]{1,0:T(1,128)S(1)}, u32[]{:S(2)}, u32[]{:S(2)}) collective-permute-start(f32[1,512]{1,0:T(1,128)S(1)} %get-tuple-element.20.refs_0_), channel_id=1, source_target_pairs={{1,0},{2,1},{3,2},{0,3},{5,4},{6,5},{7,6},{4,7},{9,8},{10,9},{11,1... | collective-permute-start | bytes 6152 | tf_op jit(solution)/shard_map/ppermute | solution.py:475

commit v2 on v1

--- a/solution.py
+++ b/solution.py
@@ -329,30 +329,40 @@
     )(q, k, v, fading, pace, even, odd)
 
 
+def fetch_kernel(*refs):
+    count = len(refs) // 2
+    *refs, sems = refs
+    copies = [
+        pltpu.make_async_copy(source, target, sems.at[n])
+        for n, (source, target) in enumerate(zip(refs[:count], refs[count:]))
+    ]
+    for copy in copies:
+        copy.start()
+    for copy in copies:
+        copy.wait()
+
+
+def fetched(*arrays):
+    return pl.pallas_call(
+        fetch_kernel,
+        in_specs=[pl.BlockSpec(memory_space=pl.ANY)] * len(arrays),
+        out_specs=[pl.BlockSpec(memory_space=pltpu.VMEM)] * len(arrays),
+        out_shape=[jax.ShapeDtypeStruct(array.shape, array.dtype) for array in arrays],
+        scratch_shapes=[pltpu.SemaphoreType.DMA((len(arrays),))],
+        compiler_params=pltpu.CompilerParams(vmem_limit_bytes=8 << 20),
+        cost_estimate=pl.CostEstimate(flops=0, bytes_accessed=9 << 20, transcendentals=0),
+        name="fetched",
+    )(*arrays)
+
+
 def outside_kernel(
-    q_hbm, low_hbm, own_hbm, high_ref, other_ref, factor_ref, out_ref, squares_ref, q_ref, low_ref, own_ref, sum_ref, sems
+    q_ref, low_ref, own_ref, high_ref, other_ref, factor_ref, out_ref, squares_ref, sum_ref
 ):
     mine = core_index()
     width = GROUP * HEAD_DIM
     half = GROUPS // 2
-    own_copy = pltpu.make_async_copy(own_hbm, own_ref, sems.at[2 * GROUPS])
-    own_copy.start()
-
-    def copies(g, low):
-        lanes = pl.ds(pl.multiple_of(g * width, width), width)
-        found = [pltpu.make_async_copy(q_hbm.at[:, lanes], q_ref.at[g], sems.at[g])]
-        if low:
-            found.append(pltpu.make_async_copy(low_hbm.at[:, lanes], low_ref.at[g], sems.at[GROUPS + g]))
-        return found
-
-    for g in range(GROUPS):
-        for copy in copies(g, g < half):
-            copy.start()
-    own_copy.wait()
 
     def group(g, low):
-        for copy in copies(g, low):
-            copy.wait()
         columns = pltpu.roll(factor_ref[...], lax.rem(128 - g * GROUP, 128), axis=1)
         rows = pl.ds(pl.multiple_of(g * 8, 8), 8)
         own, other = (
@@ -362,19 +372,16 @@
         even = jnp.where(mine == 0, own, other).reshape(16, 2, 8, 128)
         odd = jnp.where(mine == 0, other, own).reshape(16, 2, 8, 128)
         states = shuffle([even[:, 0], odd[:, 0], even[:, 1], odd[:, 1]])
-        start = g * width if low else (g - half) * width
+        before_ref, start = (low_ref, 0) if low else (high_ref, half)
         total = None
         for i in range(GROUP):
-            lanes = slice(i * HEAD_DIM, (i + 1) * HEAD_DIM)
             high, low_part = split(states[i].reshape(HEAD_DIM, HEAD_DIM))
-            q = q_ref[g, :, lanes]
+            here = pl.ds(pl.multiple_of(g * width + i * HEAD_DIM, HEAD_DIM), HEAD_DIM)
+            there = pl.ds(pl.multiple_of((g - start) * width + i * HEAD_DIM, HEAD_DIM), HEAD_DIM)
+            q = q_ref[:, here]
             carried = dot(jnp.concatenate([q, q], axis=1), jnp.concatenate([high, low_part], axis=0))
-            if low:
-                before = low_ref[g, :, lanes]
-            else:
-                before = high_ref[:, pl.ds(pl.multiple_of(start + i * HEAD_DIM, HEAD_DIM), HEAD_DIM)]
-            out = before + columns[:, i : i + 1] * carried
-            out_ref[:, pl.ds(pl.multiple_of(g * width + i * HEAD_DIM, HEAD_DIM), HEAD_DIM)] = out
+            out = before_ref[:, there] + columns[:, i : i + 1] * carried
+            out_ref[:, here] = out
             total = out * out if total is None else total + out * out
         return total
 
@@ -393,25 +400,17 @@
     squares_ref[...] = jnp.sum(sum_ref[...].T, axis=0, keepdims=True)
 
 
-def outside(q, before_low, before_high, own, other, factor):
-    width = GROUP * HEAD_DIM
-    half = GROUPS // 2
+def outside(q, before_low, own, before_high, other, factor):
     here = pl.BlockSpec(memory_space=pltpu.VMEM)
     return pl.pallas_call(
         outside_kernel,
-        in_specs=[pl.BlockSpec(memory_space=pl.ANY)] * 3 + [here] * 3,
+        in_specs=[here] * 6,
         out_specs=[here, here],
         out_shape=[
             jax.ShapeDtypeStruct((TOKENS_HERE, HEADS_HERE * HEAD_DIM), F32),
             jax.ShapeDtypeStruct((1, TOKENS_HERE), F32),
         ],
-        scratch_shapes=[
-            pltpu.VMEM((GROUPS, TOKENS_HERE, width), BF16),
-            pltpu.VMEM((half, TOKENS_HERE, width), F32),
-            pltpu.VMEM(own.shape, F32),
-            pltpu.VMEM((TOKENS_HERE, 128), F32),
-            pltpu.SemaphoreType.DMA((2 * GROUPS + 1,)),
-        ],
+        scratch_shapes=[pltpu.VMEM((TOKENS_HERE, 128), F32)],
         compiler_params=pltpu.CompilerParams(vmem_limit_bytes=24 << 20),
         cost_estimate=pl.CostEstimate(
             flops=600_000_000, bytes_accessed=11 << 20, transcendentals=0
@@ -508,7 +507,8 @@
     )
     (before_high,) = inside(*arguments, half, half, False)
     other = lax.ppermute(own, SEQ, swap)
-    out, squares = outside(q, before_low, before_high, own, other, factor)
+    near = fetched(q, before_low, own)
+    out, squares = outside(*near, before_high, other, factor)
     squares = [squares, *(turned(squares, by) for by in (1, 3, 2))]
     return normed(out, squares, gain.reshape(1, -1)), final
 

time: 83 us -> 83.8 us (level)
    pallas_call x1 -> x2, Pallas kernels: 4.05 us -> 4.84 us  [the longest x1 2.59 us: outside(): pl.pallas_call(outside_kernel, in_specs=[here] * 6, out_specs=[here, here...]
  transfers between devices with their start and end apart: 7 -> 7, of which waited for: 4 -> 4; matrix products, arithmetic and copies ran while one was open for 0% -> 0% of each run, Pallas kernels for 15% -> 17%
where the time goes in v2:
time: 83.8 us; the launch traced here: 83.5 us
  blocking collectives  26.5 us (32%)
  Pallas kernels  23.2 us (28%)
  waiting for transfers between devices  19.2 us (23%)
  starting transfers between devices  12.5 us (15%)
  local copies, waits for them, and re-layouts  1.32 us (2%)
    all_to_all x1, blocking collectives, layer(): lax.all_to_all(chip.reshape(CHIP_COUNT, PIECE + 1, 1, 128), SEQ, 0, 0, ax...  26.5 us
    all_to_all x1, waiting for transfers between devices, layer(): lax.all_to_all(prior.reshape(CHIP_COUNT, PIECE, 128), SEQ, 0, 0, axis_ind...  12.5 us
    pallas_call x2, Pallas kernels, inside(): pl.pallas_call(functools.partial(inside_kernel, first), grid=(heads // GR...  12 us
    all_to_all x1, starting transfers between devices, layer(): lax.all_to_all(prior.reshape(CHIP_COUNT, PIECE, 128), SEQ, 0, 0, axis_ind...  8.74 us
    ppermute x3, waiting for transfers between devices, turned(): lax.ppermute(value, 'tp', [((i + by) % count, i) for i in range(count)])  4.79 us
    ppermute x3, starting transfers between devices, turned(): lax.ppermute(value, 'tp', [((i + by) % count, i) for i in range(count)])  3.59 us
    pallas_call x1, Pallas kernels, local_states(): pl.pallas_call(state_kernel, in_specs=[pl.BlockSpec(memory_space=pl.ANY)]...  3.55 us
    pallas_call x1, Pallas kernels, outside(): pl.pallas_call(outside_kernel, in_specs=[here] * 6, out_specs=[here, here...  2.59 us
  transfers between devices with their start and end apart: 7, of which 4 were waited for; matrix products, arithmetic and copies ran while one was open for 0% of the time, Pallas kernels for 17%

profile of v2, /device:TPU:6, one launch (start us, length us, event | category | flops | bytes accessed | tf_op | source)
XLA Modules:
  0.0 83.5 jit_solution(8841492341515000936)
XLA Ops:
  0.6 3.6 %local_states.1 = (f32[1032,128]{1,0:T(8,128)S(1)}, f32[1032,128]{1,0:T(8,128)S(1)}) custom-call(bf16[512,2048]{1,0:T(8,128)(2,1)} %k_ref.3, bf16[512,2048]{1,0:T(8,128)(2,1)} %v_ref.3, f32[16,512]{1,0:T(8,128)} %bitcast.9, f32[1,16]{1,0:T(1,128)} %bitcast.12), custom_call_target="tpu_custom_call" | custom-call | flops 600000000 | bytes 6291456 | tf_op jit(solution)/shard_map/local_states/pallas_call | solution.py:161
  4.2 0.1 collective-permute-start
  4.3 1.9 %collective-permute-done.other_ref.odd_ref = f32[1032,128]{1,0:T(8,128)S(1)} collective-permute-done((f32[1032,128]{1,0:T(8,128)S(1)}, f32[1032,128]{1,0:T(8,128)S(1)}, u32[]{:S(2)}, u32[]{:S(2)}) %collective-permute-start) | collective-permute-done | bytes 528416 | tf_op jit(solution)/shard_map/ppermute | solution.py:484
  6.2 0.2 chip_states.1
  6.4 26.5 %all_to_all.10 = f32[32,33,1,128]{3,2,1,0:T(1,128)S(1)} all-to-all(f32[32,33,1,128]{3,2,1,0:T(1,128)S(1)} %bitcast.7), channel_id=1, replica_groups={{248,240,232,224,216,208,200,192,184,176,168,160,152,144,136,128,120,11..., dimensions={0} | all-to-all | bytes 1081344 | tf_op jit(solution)/shard_map/all_to_all | solution.py:487
  32.9 1.0 %scan_chips.1 = (f32[1024,128]{1,0:T(8,128)}, f32[16,256]{1,0:T(8,128)}) custom-call(f32[1056,128]{1,0:T(8,128)S(1)} %bitcast.6), custom_call_target="tpu_custom_call" | custom-call | flops 524288 | bytes 1048576 | tf_op jit(solution)/shard_map/scan_chips/pallas_call | solution.py:229
  33.9 8.7 %all-to-all-start.1 = ((f32[32,32,128]{2,1,0:T(8,128)}), f32[32,32,128]{2,1,0:T(8,128)S(1)}, u32[]{:S(2)}, u32[]{:S(2)}) async-start(f32[32,32,128]{2,1,0:T(8,128)} %bitcast.4), calls=%async_computation.1 | async-start | bytes 1048576 | tf_op jit(solution)/shard_map/all_to_all | solution.py:500
  42.6 0.1 collective-permute-start.1
  42.7 12.5 %all-to-all-done.1.refs_2_ = f32[32,32,128]{2,1,0:T(8,128)S(1)} async-done(((f32[32,32,128]{2,1,0:T(8,128)}), f32[32,32,128]{2,1,0:T(8,128)S(1)}, u32[]{:S(2)}, u32[]{:S(2)}) %all-to-all-start.1) | async-done | bytes 524320 | tf_op jit(solution)/shard_map/all_to_all | solution.py:500
  55.3 0.0 collective-permute-start.2
  55.3 0.0 collective-permute-done.1.even_ref
  55.3 6.0 %inside.3.high_ref = f32[512,1024]{1,0:T(8,128)S(1)} custom-call(bf16[512,2048]{1,0:T(8,128)(2,1)} %q_ref.3, bf16[512,2048]{1,0:T(8,128)(2,1)} %k_ref.3, bf16[512,2048]{1,0:T(8,128)(2,1)} %v_ref.3, f32[16,512]{1,0:T(8,128)} %bitcast.10, f32[1,16]{1,0:T(1,128)} %bitcast.13, f32[1032,128]{1,0:T(8,128)S(1)} %collective-permute-done.1.even_ref, ...), custom_call_target="tpu_custom_call" | custom-call | flops 1000000000 | bytes 6291456 | tf_op jit(solution)/shard_map/inside/pallas_call | solution.py:306
  61.3 6.0 %inside.2 = (f32[512,1024]{1,0:T(8,128)S(1)}, f32[512,128]{1,0:T(8,128)S(1)}) custom-call(bf16[512,2048]{1,0:T(8,128)(2,1)} %q_ref.3, bf16[512,2048]{1,0:T(8,128)(2,1)} %k_ref.3, bf16[512,2048]{1,0:T(8,128)(2,1)} %v_ref.3, f32[16,512]{1,0:T(8,128)} %bitcast.11, f32[1,16]{1,0:T(1,128)} %bitcast.14, f32[1032,128]{1,0:T(8,128)S(1)} %collective-permute-done.1.even_ref, ...), custom_call_target="tpu_custom_call" | custom-call | flops 1000000000 | bytes 6291456 | tf_op jit(solution)/shard_map/inside/pallas_call | solution.py:306
  67.4 0.0 copy-start
  67.4 1.3 %copy-done = f32[512,1024]{1,0:T(8,128)} copy-done((f32[512,1024]{1,0:T(8,128)}, f32[512,1024]{1,0:T(8,128)S(1)}, u32[]{:S(2)}) %copy-start) | copy-done | bytes 2097176
  68.7 2.2 %fetched.1 = (bf16[512,2048]{1,0:T(8,128)(2,1)S(1)}, f32[512,1024]{1,0:T(8,128)S(1)}, f32[32,32,128]{2,1,0:T(8,128)S(1)}) custom-call(bf16[512,2048]{1,0:T(8,128)(2,1)} %q_ref.3, f32[512,1024]{1,0:T(8,128)} %copy-done, f32[32,32,128]{2,1,0:T(8,128)S(1)} %all-to-all-done.1.refs_2_), custom_call_target="tpu_custom_call" | custom-call | bytes 9437184 | tf_op jit(solution)/shard_map/fetched/pallas_call | solution.py:346
  70.9 0.0 collective-permute-done.2.other_ref
  70.9 0.0 copy-start.1
  71.0 2.6 %outside.1 = (f32[512,2048]{1,0:T(8,128)S(1)}, f32[1,512]{1,0:T(1,128)S(1)}) custom-call(bf16[512,2048]{1,0:T(8,128)(2,1)S(1)} %get-tuple-element.21.q_ref, f32[512,1024]{1,0:T(8,128)S(1)} %get-tuple-element.22.low_ref, f32[32,32,128]{2,1,0:T(8,128)S(1)} %get-tuple-element.23.own_ref, f32[512,1024]{1,0:T(8,128)S(1)} %inside.3.high_ref, ...), custom_call_target="tpu_custom_call" | custom-call | flops 600000000 | bytes 11534336 | tf_op jit(solution)/shard_map/outside/pallas_call | solution.py:405
  73.6 1.5 %collective-permute-start.5 = (f32[1,512]{1,0:T(1,128)S(1)}, f32[1,512]{1,0:T(1,128)S(1)}, u32[]{:S(2)}, u32[]{:S(2)}) collective-permute-start(f32[1,512]{1,0:T(1,128)S(1)} %get-tuple-element.26.refs_0_), channel_id=1, source_target_pairs={{2,0},{3,1},{0,2},{1,3},{6,4},{7,5},{4,6},{5,7},{10,8},{11,9},{8,1... | collective-permute-start | bytes 6152 | tf_op jit(solution)/shard_map/ppermute | solution.py:474
  75.0 2.1 %collective-permute-start.4 = (f32[1,512]{1,0:T(1,128)S(1)}, f32[1,512]{1,0:T(1,128)S(1)}, u32[]{:S(2)}, u32[]{:S(2)}) collective-permute-start(f32[1,512]{1,0:T(1,128)S(1)} %get-tuple-element.26.refs_0_), channel_id=1, source_target_pairs={{3,0},{0,1},{1,2},{2,3},{7,4},{4,5},{5,6},{6,7},{11,8},{8,9},{9,10... | collective-permute-start | bytes 6152 | tf_op jit(solution)/shard_map/ppermute | solution.py:474
  77.1 1.6 %collective-permute-done.5.refs_3_ = f32[1,512]{1,0:T(1,128)S(1)} collective-permute-done((f32[1,512]{1,0:T(1,128)S(1)}, f32[1,512]{1,0:T(1,128)S(1)}, u32[]{:S(2)}, u32[]{:S(2)}) %collective-permute-start.5) | collective-permute-done | bytes 2080 | tf_op jit(solution)/shard_map/ppermute | solution.py:474
  78.7 3.2 %collective-permute-done.3.refs_1_ = f32[1,512]{1,0:T(1,128)S(1)} collective-permute-done((f32[1,512]{1,0:T(1,128)S(1)}, f32[1,512]{1,0:T(1,128)S(1)}, u32[]{:S(2)}, u32[]{:S(2)}) %collective-permute-start.3) | collective-permute-done | bytes 2080 | tf_op jit(solution)/shard_map/ppermute | solution.py:474
  81.9 1.6 %normed.1 = bf16[512,2048]{1,0:T(8,128)(2,1)} custom-call(f32[512,2048]{1,0:T(8,128)S(1)} %get-tuple-element.25.out_ref, f32[1,512]{1,0:T(1,128)S(1)} %get-tuple-element.26.refs_0_, f32[1,512]{1,0:T(1,128)S(1)} %collective-permute-done.3.refs_1_, f32[1,512]{1,0:T(1,128)S(1)} %collective-permute-done.4.refs_2_, f32[1,512]{1,0:T(1,128)S(1)} %collective-permute-done.5.refs_3_, ...), custom_call_target="tpu_custom_call" | custom-call | flops 2097152 | bytes 6291456 | tf_op jit(solution)/shard_map/normed/pallas_call | solution.py:456
  (3 shorter events, 0.0 us)
Async XLA Ops:
  4.2 2.0 %collective-permute-start = (f32[1032,128]{1,0:T(8,128)S(1)}, f32[1032,128]{1,0:T(8,128)S(1)}, u32[]{:S(2)}, u32[]{:S(2)}) collective-permute-start(f32[1032,128]{1,0:T(8,128)S(1)} %get-tuple-element.16), channel_id=1, source_target_pairs={{0,4},{4,0},{8,12},{12,8},{16,20},{20,16},{24,28},{28,24},{32,36},... | collective-permute-start | bytes 1585160 | tf_op jit(solution)/shard_map/ppermute | solution.py:484
  33.9 21.4 %all-to-all-start.1 = ((f32[32,32,128]{2,1,0:T(8,128)}), f32[32,32,128]{2,1,0:T(8,128)S(1)}, u32[]{:S(2)}, u32[]{:S(2)}) async-start(f32[32,32,128]{2,1,0:T(8,128)} %bitcast.4), calls=%async_computation.1 | async-start | bytes 1048576 | tf_op jit(solution)/shard_map/all_to_all | solution.py:500
  42.6 12.7 %collective-permute-start.1 = (f32[1032,128]{1,0:T(8,128)S(1)}, f32[1032,128]{1,0:T(8,128)S(1)}, u32[]{:S(2)}, u32[]{:S(2)}) collective-permute-start(f32[1032,128]{1,0:T(8,128)S(1)} %get-tuple-element.17), channel_id=1, source_target_pairs={{0,4},{4,0},{8,12},{12,8},{16,20},{20,16},{24,28},{28,24},{32,36},... | collective-permute-start | bytes 1585160 | tf_op jit(solution)/shard_map/ppermute | solution.py:486
  55.3 15.7 %collective-permute-start.2 = (f32[32,32,128]{2,1,0:T(8,128)S(1)}, f32[32,32,128]{2,1,0:T(8,128)S(1)}, u32[]{:S(2)}, u32[]{:S(2)}) collective-permute-start(f32[32,32,128]{2,1,0:T(8,128)S(1)} %all-to-all-done.1.refs_2_), channel_id=1, source_target_pairs={{0,4},{4,0},{8,12},{12,8},{16,20},{20,16},{24,28},{28,24},{32,36},... | collective-permute-start | bytes 1572872 | tf_op jit(solution)/shard_map/ppermute | solution.py:509
  67.4 1.3 %copy-start = (f32[512,1024]{1,0:T(8,128)}, f32[512,1024]{1,0:T(8,128)S(1)}, u32[]{:S(2)}) copy-start(f32[512,1024]{1,0:T(8,128)S(1)} %get-tuple-element.18.refs_1_) | copy-start | bytes 6291460
  70.9 11.0 %copy-start.1 = (f32[2048]{0:T(1024)S(1)}, f32[2048]{0:T(1024)}, u32[]{:S(2)}) copy-start(f32[2048]{0:T(1024)} %param.11) | copy-start | bytes 24580
  73.6 5.2 %collective-permute-start.5 = (f32[1,512]{1,0:T(1,128)S(1)}, f32[1,512]{1,0:T(1,128)S(1)}, u32[]{:S(2)}, u32[]{:S(2)}) collective-permute-start(f32[1,512]{1,0:T(1,128)S(1)} %get-tuple-element.26.refs_0_), channel_id=1, source_target_pairs={{2,0},{3,1},{0,2},{1,3},{6,4},{7,5},{4,6},{5,7},{10,8},{11,9},{8,1... | collective-permute-start | bytes 6152 | tf_op jit(solution)/shard_map/ppermute | solution.py:474
  75.0 3.7 %collective-permute-start.4 = (f32[1,512]{1,0:T(1,128)S(1)}, f32[1,512]{1,0:T(1,128)S(1)}, u32[]{:S(2)}, u32[]{:S(2)}) collective-permute-start(f32[1,512]{1,0:T(1,128)S(1)} %get-tuple-element.26.refs_0_), channel_id=1, source_target_pairs={{3,0},{0,1},{1,2},{2,3},{7,4},{4,5},{5,6},{6,7},{11,8},{8,9},{9,10... | collective-permute-start | bytes 6152 | tf_op jit(solution)/shard_map/ppermute | solution.py:474
  77.1 4.8 %collective-permute-start.3 = (f32[1,512]{1,0:T(1,128)S(1)}, f32[1,512]{1,0:T(1,128)S(1)}, u32[]{:S(2)}, u32[]{:S(2)}) collective-permute-start(f32[1,512]{1,0:T(1,128)S(1)} %get-tuple-element.26.refs_0_), channel_id=1, source_target_pairs={{1,0},{2,1},{3,2},{0,3},{5,4},{6,5},{7,6},{4,7},{9,8},{10,9},{11,1... | collective-permute-start | bytes 6152 | tf_op jit(solution)/shard_map/ppermute | solution.py:474

commit v3 on v2

--- a/solution.py
+++ b/solution.py
@@ -329,12 +329,12 @@
     )(q, k, v, fading, pace, even, odd)
 
 
-def fetch_kernel(*refs):
-    count = len(refs) // 2
-    *refs, sems = refs
+def fetch_kernel(q_hbm, own_hbm, low_hbm, q_ref, own_ref, low_ref, sems):
+    first = low_hbm.at[:, pl.ds(0, GROUP * HEAD_DIM)]
+    pairs = ((own_hbm, own_ref), (q_hbm, q_ref), (first, low_ref))
     copies = [
         pltpu.make_async_copy(source, target, sems.at[n])
-        for n, (source, target) in enumerate(zip(refs[:count], refs[count:]))
+        for n, (source, target) in enumerate(pairs)
     ]
     for copy in copies:
         copy.start()
@@ -342,28 +342,36 @@
         copy.wait()
 
 
-def fetched(*arrays):
+def fetched(q, own, before_low):
+    group = (TOKENS_HERE, GROUP * HEAD_DIM)
     return pl.pallas_call(
         fetch_kernel,
-        in_specs=[pl.BlockSpec(memory_space=pl.ANY)] * len(arrays),
-        out_specs=[pl.BlockSpec(memory_space=pltpu.VMEM)] * len(arrays),
-        out_shape=[jax.ShapeDtypeStruct(array.shape, array.dtype) for array in arrays],
-        scratch_shapes=[pltpu.SemaphoreType.DMA((len(arrays),))],
+        in_specs=[pl.BlockSpec(memory_space=pl.ANY)] * 3,
+        out_specs=[pl.BlockSpec(memory_space=pltpu.VMEM)] * 3,
+        out_shape=[
+            jax.ShapeDtypeStruct(q.shape, BF16),
+            jax.ShapeDtypeStruct(own.shape, F32),
+            jax.ShapeDtypeStruct(group, F32),
+        ],
+        scratch_shapes=[pltpu.SemaphoreType.DMA((3,))],
         compiler_params=pltpu.CompilerParams(vmem_limit_bytes=8 << 20),
-        cost_estimate=pl.CostEstimate(flops=0, bytes_accessed=9 << 20, transcendentals=0),
+        cost_estimate=pl.CostEstimate(flops=0, bytes_accessed=7 << 20, transcendentals=0),
         name="fetched",
-    )(*arrays)
+    )(q, own, before_low)
 
 
 def outside_kernel(
-    q_ref, low_ref, own_ref, high_ref, other_ref, factor_ref, out_ref, squares_ref, sum_ref
+    q_ref, own_ref, first_ref, low_hbm, high_ref, other_ref, factor_ref, out_ref, squares_ref, sum_ref, second_ref, sem
 ):
+    second = low_hbm.at[:, pl.ds(GROUP * HEAD_DIM, GROUP * HEAD_DIM)]
+    copy = pltpu.make_async_copy(second, second_ref, sem)
+    copy.start()
     mine = core_index()
     width = GROUP * HEAD_DIM
     half = GROUPS // 2
 
-    def group(g, low):
-        columns = pltpu.roll(factor_ref[...], lax.rem(128 - g * GROUP, 128), axis=1)
+    def group(g, before_ref, start):
+        columns = pltpu.roll(factor_ref[...], (128 - g * GROUP) % 128, axis=1)
         rows = pl.ds(pl.multiple_of(g * 8, 8), 8)
         own, other = (
             jnp.stack([ref[place(p, BACK_REVERSED), rows, :] for p in range(CHIP_COUNT)])
@@ -372,7 +380,6 @@
         even = jnp.where(mine == 0, own, other).reshape(16, 2, 8, 128)
         odd = jnp.where(mine == 0, other, own).reshape(16, 2, 8, 128)
         states = shuffle([even[:, 0], odd[:, 0], even[:, 1], odd[:, 1]])
-        before_ref, start = (low_ref, 0) if low else (high_ref, half)
         total = None
         for i in range(GROUP):
             high, low_part = split(states[i].reshape(HEAD_DIM, HEAD_DIM))
@@ -387,36 +394,38 @@
 
     sum_ref[...] = jnp.zeros_like(sum_ref)
 
-    def low_group(g, carry):
-        sum_ref[...] += group(g, True)
+    def high_group(g, carry):
+        sum_ref[...] += group(g, high_ref, half)
         return carry
 
-    def high_group(g, carry):
-        sum_ref[...] += group(g, False)
-        return carry
-
-    lax.fori_loop(0, half, low_group, 0)
     lax.fori_loop(half, GROUPS, high_group, 0)
+    sum_ref[...] += group(0, first_ref, 0)
+    copy.wait()
+    sum_ref[...] += group(1, second_ref, 1)
     squares_ref[...] = jnp.sum(sum_ref[...].T, axis=0, keepdims=True)
 
 
-def outside(q, before_low, own, before_high, other, factor):
+def outside(q, own, first, before_low, before_high, other, factor):
     here = pl.BlockSpec(memory_space=pltpu.VMEM)
     return pl.pallas_call(
         outside_kernel,
-        in_specs=[here] * 6,
+        in_specs=[here] * 3 + [pl.BlockSpec(memory_space=pl.ANY)] + [here] * 3,
         out_specs=[here, here],
         out_shape=[
             jax.ShapeDtypeStruct((TOKENS_HERE, HEADS_HERE * HEAD_DIM), F32),
             jax.ShapeDtypeStruct((1, TOKENS_HERE), F32),
         ],
-        scratch_shapes=[pltpu.VMEM((TOKENS_HERE, 128), F32)],
+        scratch_shapes=[
+            pltpu.VMEM((TOKENS_HERE, 128), F32),
+            pltpu.VMEM((TOKENS_HERE, GROUP * HEAD_DIM), F32),
+            pltpu.SemaphoreType.DMA,
+        ],
         compiler_params=pltpu.CompilerParams(vmem_limit_bytes=24 << 20),
         cost_estimate=pl.CostEstimate(
             flops=600_000_000, bytes_accessed=11 << 20, transcendentals=0
         ),
         name="outside",
-    )(q, before_low, own, before_high, other, factor)
+    )(q, own, first, before_low, before_high, other, factor)
 
 
 NORM_ROWS = 64
@@ -507,8 +516,8 @@
     )
     (before_high,) = inside(*arguments, half, half, False)
     other = lax.ppermute(own, SEQ, swap)
-    near = fetched(q, before_low, own)
-    out, squares = outside(*near, before_high, other, factor)
+    near = fetched(q, own, before_low)
+    out, squares = outside(*near, before_low, before_high, other, factor)
     squares = [squares, *(turned(squares, by) for by in (1, 3, 2))]
     return normed(out, squares, gain.reshape(1, -1)), final
 

time: 83.8 us -> 83.2 us (level)
  no operation moved by 1% of the time
where the time goes in v3:
time: 83.2 us; the launch traced here: 82.9 us
  blocking collectives  26.5 us (32%)
  Pallas kernels  22.6 us (27%)
  waiting for transfers between devices  19.2 us (23%)
  starting transfers between devices  12.5 us (15%)
  local copies, waits for them, and re-layouts  1.32 us (2%)
    all_to_all x1, blocking collectives, layer(): lax.all_to_all(chip.reshape(CHIP_COUNT, PIECE + 1, 1, 128), SEQ, 0, 0, ax...  26.5 us
    all_to_all x1, waiting for transfers between devices, layer(): lax.all_to_all(prior.reshape(CHIP_COUNT, PIECE, 128), SEQ, 0, 0, axis_ind...  12.5 us
    pallas_call x2, Pallas kernels, inside(): pl.pallas_call(functools.partial(inside_kernel, first), grid=(heads // GR...  12 us
    all_to_all x1, starting transfers between devices, layer(): lax.all_to_all(prior.reshape(CHIP_COUNT, PIECE, 128), SEQ, 0, 0, axis_ind...  8.74 us
    ppermute x3, waiting for transfers between devices, turned(): lax.ppermute(value, 'tp', [((i + by) % count, i) for i in range(count)])  4.79 us
    ppermute x3, starting transfers between devices, turned(): lax.ppermute(value, 'tp', [((i + by) % count, i) for i in range(count)])  3.59 us
    pallas_call x1, Pallas kernels, local_states(): pl.pallas_call(state_kernel, in_specs=[pl.BlockSpec(memory_space=pl.ANY)]...  3.55 us
    pallas_call x1, Pallas kernels, outside(): pl.pallas_call(outside_kernel, in_specs=[here] * 3 + [pl.BlockSpec(memory...  2.31 us
  transfers between devices with their start and end apart: 7, of which 4 were waited for; matrix products, arithmetic and copies ran while one was open for 0% of the time, Pallas kernels for 17%

profile of v3, /device:TPU:6, one launch (start us, length us, event | category | flops | bytes accessed | tf_op | source)
XLA Modules:
  0.0 82.9 jit_solution(12735892792684504275)
XLA Ops:
  0.6 3.6 %local_states.1 = (f32[1032,128]{1,0:T(8,128)S(1)}, f32[1032,128]{1,0:T(8,128)S(1)}) custom-call(bf16[512,2048]{1,0:T(8,128)(2,1)} %k_ref.3, bf16[512,2048]{1,0:T(8,128)(2,1)} %v_ref.3, f32[16,512]{1,0:T(8,128)} %bitcast.9, f32[1,16]{1,0:T(1,128)} %bitcast.12), custom_call_target="tpu_custom_call" | custom-call | flops 600000000 | bytes 6291456 | tf_op jit(solution)/shard_map/local_states/pallas_call | solution.py:161
  4.2 0.1 collective-permute-start
  4.3 1.9 %collective-permute-done.other_ref.odd_ref = f32[1032,128]{1,0:T(8,128)S(1)} collective-permute-done((f32[1032,128]{1,0:T(8,128)S(1)}, f32[1032,128]{1,0:T(8,128)S(1)}, u32[]{:S(2)}, u32[]{:S(2)}) %collective-permute-start) | collective-permute-done | bytes 528416 | tf_op jit(solution)/shard_map/ppermute | solution.py:493
  6.2 0.2 chip_states.1
  6.4 26.5 %all_to_all.10 = f32[32,33,1,128]{3,2,1,0:T(1,128)S(1)} all-to-all(f32[32,33,1,128]{3,2,1,0:T(1,128)S(1)} %bitcast.7), channel_id=1, replica_groups={{248,240,232,224,216,208,200,192,184,176,168,160,152,144,136,128,120,11..., dimensions={0} | all-to-all | bytes 1081344 | tf_op jit(solution)/shard_map/all_to_all | solution.py:496
  32.9 1.0 %scan_chips.1 = (f32[1024,128]{1,0:T(8,128)}, f32[16,256]{1,0:T(8,128)}) custom-call(f32[1056,128]{1,0:T(8,128)S(1)} %bitcast.6), custom_call_target="tpu_custom_call" | custom-call | flops 524288 | bytes 1048576 | tf_op jit(solution)/shard_map/scan_chips/pallas_call | solution.py:229
  33.9 8.7 %all-to-all-start.1 = ((f32[32,32,128]{2,1,0:T(8,128)}), f32[32,32,128]{2,1,0:T(8,128)S(1)}, u32[]{:S(2)}, u32[]{:S(2)}) async-start(f32[32,32,128]{2,1,0:T(8,128)} %bitcast.4), calls=%async_computation.1 | async-start | bytes 1048576 | tf_op jit(solution)/shard_map/all_to_all | solution.py:509
  42.6 0.1 collective-permute-start.1
  42.7 12.5 %all-to-all-done.1.own_hbm = f32[32,32,128]{2,1,0:T(8,128)S(1)} async-done(((f32[32,32,128]{2,1,0:T(8,128)}), f32[32,32,128]{2,1,0:T(8,128)S(1)}, u32[]{:S(2)}, u32[]{:S(2)}) %all-to-all-start.1) | async-done | bytes 524320 | tf_op jit(solution)/shard_map/all_to_all | solution.py:509
  55.3 0.0 collective-permute-start.2
  55.3 0.0 collective-permute-done.1.even_ref
  55.3 6.0 %inside.3.high_ref = f32[512,1024]{1,0:T(8,128)S(1)} custom-call(bf16[512,2048]{1,0:T(8,128)(2,1)} %q_ref.3, bf16[512,2048]{1,0:T(8,128)(2,1)} %k_ref.3, bf16[512,2048]{1,0:T(8,128)(2,1)} %v_ref.3, f32[16,512]{1,0:T(8,128)} %bitcast.10, f32[1,16]{1,0:T(1,128)} %bitcast.13, f32[1032,128]{1,0:T(8,128)S(1)} %collective-permute-done.1.even_ref, ...), custom_call_target="tpu_custom_call" | custom-call | flops 1000000000 | bytes 6291456 | tf_op jit(solution)/shard_map/inside/pallas_call | solution.py:306
  61.3 6.0 %inside.2 = (f32[512,1024]{1,0:T(8,128)S(1)}, f32[512,128]{1,0:T(8,128)S(1)}) custom-call(bf16[512,2048]{1,0:T(8,128)(2,1)} %q_ref.3, bf16[512,2048]{1,0:T(8,128)(2,1)} %k_ref.3, bf16[512,2048]{1,0:T(8,128)(2,1)} %v_ref.3, f32[16,512]{1,0:T(8,128)} %bitcast.11, f32[1,16]{1,0:T(1,128)} %bitcast.14, f32[1032,128]{1,0:T(8,128)S(1)} %collective-permute-done.1.even_ref, ...), custom_call_target="tpu_custom_call" | custom-call | flops 1000000000 | bytes 6291456 | tf_op jit(solution)/shard_map/inside/pallas_call | solution.py:306
  67.4 0.0 copy-start
  67.4 1.3 %copy-done = f32[512,1024]{1,0:T(8,128)} copy-done((f32[512,1024]{1,0:T(8,128)}, f32[512,1024]{1,0:T(8,128)S(1)}, u32[]{:S(2)}) %copy-start) | copy-done | bytes 2097176
  68.7 1.9 %fetched.1 = (bf16[512,2048]{1,0:T(8,128)(2,1)S(1)}, f32[32,32,128]{2,1,0:T(8,128)S(1)}, f32[512,512]{1,0:T(8,128)S(1)}) custom-call(bf16[512,2048]{1,0:T(8,128)(2,1)} %q_ref.3, f32[32,32,128]{2,1,0:T(8,128)S(1)} %all-to-all-done.1.own_hbm, f32[512,1024]{1,0:T(8,128)} %copy-done), custom_call_target="tpu_custom_call" | custom-call | bytes 7340032 | tf_op jit(solution)/shard_map/fetched/pallas_call | solution.py:347
  70.6 0.0 copy-start.1
  70.6 2.3 %outside.1 = (f32[512,2048]{1,0:T(8,128)S(1)}, f32[1,512]{1,0:T(1,128)S(1)}) custom-call(bf16[512,2048]{1,0:T(8,128)(2,1)S(1)} %get-tuple-element.21.q_ref, f32[32,32,128]{2,1,0:T(8,128)S(1)} %get-tuple-element.22.own_ref, f32[512,512]{1,0:T(8,128)S(1)} %get-tuple-element.23.first_ref, f32[512,1024]{1,0:T(8,128)} %copy-done, ...), custom_call_target="tpu_custom_call" | custom-call | flops 600000000 | bytes 11534336 | tf_op jit(solution)/shard_map/outside/pallas_call | solution.py:410
  72.9 1.5 %collective-permute-start.5 = (f32[1,512]{1,0:T(1,128)S(1)}, f32[1,512]{1,0:T(1,128)S(1)}, u32[]{:S(2)}, u32[]{:S(2)}) collective-permute-start(f32[1,512]{1,0:T(1,128)S(1)} %get-tuple-element.26.refs_0_), channel_id=1, source_target_pairs={{2,0},{3,1},{0,2},{1,3},{6,4},{7,5},{4,6},{5,7},{10,8},{11,9},{8,1... | collective-permute-start | bytes 6152 | tf_op jit(solution)/shard_map/ppermute | solution.py:483
  74.4 2.1 %collective-permute-start.4 = (f32[1,512]{1,0:T(1,128)S(1)}, f32[1,512]{1,0:T(1,128)S(1)}, u32[]{:S(2)}, u32[]{:S(2)}) collective-permute-start(f32[1,512]{1,0:T(1,128)S(1)} %get-tuple-element.26.refs_0_), channel_id=1, source_target_pairs={{3,0},{0,1},{1,2},{2,3},{7,4},{4,5},{5,6},{6,7},{11,8},{8,9},{9,10... | collective-permute-start | bytes 6152 | tf_op jit(solution)/shard_map/ppermute | solution.py:483
  76.5 0.0 collective-permute-start.3
  76.5 1.6 %collective-permute-done.5.refs_3_ = f32[1,512]{1,0:T(1,128)S(1)} collective-permute-done((f32[1,512]{1,0:T(1,128)S(1)}, f32[1,512]{1,0:T(1,128)S(1)}, u32[]{:S(2)}, u32[]{:S(2)}) %collective-permute-start.5) | collective-permute-done | bytes 2080 | tf_op jit(solution)/shard_map/ppermute | solution.py:483
  78.1 3.2 %collective-permute-done.3.refs_1_ = f32[1,512]{1,0:T(1,128)S(1)} collective-permute-done((f32[1,512]{1,0:T(1,128)S(1)}, f32[1,512]{1,0:T(1,128)S(1)}, u32[]{:S(2)}, u32[]{:S(2)}) %collective-permute-start.3) | collective-permute-done | bytes 2080 | tf_op jit(solution)/shard_map/ppermute | solution.py:483
  81.3 1.6 %normed.1 = bf16[512,2048]{1,0:T(8,128)(2,1)} custom-call(f32[512,2048]{1,0:T(8,128)S(1)} %get-tuple-element.25.out_ref, f32[1,512]{1,0:T(1,128)S(1)} %get-tuple-element.26.refs_0_, f32[1,512]{1,0:T(1,128)S(1)} %collective-permute-done.3.refs_1_, f32[1,512]{1,0:T(1,128)S(1)} %collective-permute-done.4.refs_2_, f32[1,512]{1,0:T(1,128)S(1)} %collective-permute-done.5.refs_3_, ...), custom_call_target="tpu_custom_call" | custom-call | flops 2097152 | bytes 6291456 | tf_op jit(solution)/shard_map/normed/pallas_call | solution.py:465
  (3 shorter events, 0.0 us)
Async XLA Ops:
  4.2 2.0 %collective-permute-start = (f32[1032,128]{1,0:T(8,128)S(1)}, f32[1032,128]{1,0:T(8,128)S(1)}, u32[]{:S(2)}, u32[]{:S(2)}) collective-permute-start(f32[1032,128]{1,0:T(8,128)S(1)} %get-tuple-element.16), channel_id=1, source_target_pairs={{0,4},{4,0},{8,12},{12,8},{16,20},{20,16},{24,28},{28,24},{32,36},... | collective-permute-start | bytes 1585160 | tf_op jit(solution)/shard_map/ppermute | solution.py:493
  33.9 21.4 %all-to-all-start.1 = ((f32[32,32,128]{2,1,0:T(8,128)}), f32[32,32,128]{2,1,0:T(8,128)S(1)}, u32[]{:S(2)}, u32[]{:S(2)}) async-start(f32[32,32,128]{2,1,0:T(8,128)} %bitcast.4), calls=%async_computation.1 | async-start | bytes 1048576 | tf_op jit(solution)/shard_map/all_to_all | solution.py:509
  42.6 12.7 %collective-permute-start.1 = (f32[1032,128]{1,0:T(8,128)S(1)}, f32[1032,128]{1,0:T(8,128)S(1)}, u32[]{:S(2)}, u32[]{:S(2)}) collective-permute-start(f32[1032,128]{1,0:T(8,128)S(1)} %get-tuple-element.19), channel_id=1, source_target_pairs={{0,4},{4,0},{8,12},{12,8},{16,20},{20,16},{24,28},{28,24},{32,36},... | collective-permute-start | bytes 1585160 | tf_op jit(solution)/shard_map/ppermute | solution.py:495
  55.3 15.3 %collective-permute-start.2 = (f32[32,32,128]{2,1,0:T(8,128)S(1)}, f32[32,32,128]{2,1,0:T(8,128)S(1)}, u32[]{:S(2)}, u32[]{:S(2)}) collective-permute-start(f32[32,32,128]{2,1,0:T(8,128)S(1)} %all-to-all-done.1.own_hbm), channel_id=1, source_target_pairs={{0,4},{4,0},{8,12},{12,8},{16,20},{20,16},{24,28},{28,24},{32,36},... | collective-permute-start | bytes 1572872 | tf_op jit(solution)/shard_map/ppermute | solution.py:518
  67.4 1.3 %copy-start = (f32[512,1024]{1,0:T(8,128)}, f32[512,1024]{1,0:T(8,128)S(1)}, u32[]{:S(2)}) copy-start(f32[512,1024]{1,0:T(8,128)S(1)} %get-tuple-element.20.low_hbm) | copy-start | bytes 6291460
  70.6 10.7 %copy-start.1 = (f32[2048]{0:T(1024)S(1)}, f32[2048]{0:T(1024)}, u32[]{:S(2)}) copy-start(f32[2048]{0:T(1024)} %param.11) | copy-start | bytes 24580
  72.9 5.2 %collective-permute-start.5 = (f32[1,512]{1,0:T(1,128)S(1)}, f32[1,512]{1,0:T(1,128)S(1)}, u32[]{:S(2)}, u32[]{:S(2)}) collective-permute-start(f32[1,512]{1,0:T(1,128)S(1)} %get-tuple-element.26.refs_0_), channel_id=1, source_target_pairs={{2,0},{3,1},{0,2},{1,3},{6,4},{7,5},{4,6},{5,7},{10,8},{11,9},{8,1... | collective-permute-start | bytes 6152 | tf_op jit(solution)/shard_map/ppermute | solution.py:483
  74.4 3.7 %collective-permute-start.4 = (f32[1,512]{1,0:T(1,128)S(1)}, f32[1,512]{1,0:T(1,128)S(1)}, u32[]{:S(2)}, u32[]{:S(2)}) collective-permute-start(f32[1,512]{1,0:T(1,128)S(1)} %get-tuple-element.26.refs_0_), channel_id=1, source_target_pairs={{3,0},{0,1},{1,2},{2,3},{7,4},{4,5},{5,6},{6,7},{11,8},{8,9},{9,10... | collective-permute-start | bytes 6152 | tf_op jit(solution)/shard_map/ppermute | solution.py:483
  76.5 4.8 %collective-permute-start.3 = (f32[1,512]{1,0:T(1,128)S(1)}, f32[1,512]{1,0:T(1,128)S(1)}, u32[]{:S(2)}, u32[]{:S(2)}) collective-permute-start(f32[1,512]{1,0:T(1,128)S(1)} %get-tuple-element.26.refs_0_), channel_id=1, source_target_pairs={{1,0},{2,1},{3,2},{0,3},{5,4},{6,5},{7,6},{4,7},{9,8},{10,9},{11,1... | collective-permute-start | bytes 6152 | tf_op jit(solution)/shard_map/ppermute | solution.py:483
